TPU v7x, 32 devices: a whole 2x2x4 slice. The times are simulated.
32 devices in a mesh: replica: 4 (over y, core), shard: 8 (over z, x).
Axes of the slice: x: 2, y: 2, z: 4, core: 2. Of those that a mesh axis runs over, the one named last changes fastest.
Arguments:
- enc_delta: bfloat16 [4, 5120, 8192], P('replica', 'shard'), may hold values from -6 to 6
- enc_params: float32 [4, 8, 160, 8192], P('replica', 'shard'), may hold values from -6 to 6
- enc_momentum: float32 [4, 8, 160, 8192], P('replica', 'shard'), may hold values from -6 to 6
- dec_delta: bfloat16 [4, 5120, 8192], P('replica', 'shard'), may hold values from -6 to 6
- dec_params: float32 [4, 8, 160, 8192], P('replica', 'shard'), may hold values from -6 to 6
- dec_momentum: float32 [4, 8, 160, 8192], P('replica', 'shard'), may hold values from -6 to 6
Outputs:
- enc_params_new: float32 [4, 8, 160, 8192], P('replica', 'shard')
- enc_momentum_new: float32 [4, 8, 160, 8192], P('replica', 'shard')
- enc_working: bfloat16 [5120, 8192], P('shard')
- dec_params_new: float32 [4, 8, 160, 8192], P('replica', 'shard')
- dec_momentum_new: float32 [4, 8, 160, 8192], P('replica', 'shard')
- dec_working: bfloat16 [5120, 8192], P('shard')
All inputs are finite; a program needn't handle non-finite values.
Results may differ from a plain program's by a relative error of at most 0.007.
Values may be sent and summed in bfloat16 or wider, within the bound.
No kernel may reach another device: no remote copies, remote signals or barrier semaphores. Data moves between devices by JAX's collectives and lax.ppermute only.
A program may use at most 192 MiB of HBM per device.

v0:
```python
import jax
import jax.numpy as jnp
from jax import lax
from jax.sharding import PartitionSpec as P

outer_rate = 0.7
nesterov_keep = 0.9


def reduce_block(deltas):
    replicas = lax.axis_size("replica")
    local_rows = deltas[0]
    row_count, full_width = local_rows.shape
    slab_rows = row_count // replicas
    grouped = local_rows.reshape(replicas, slab_rows, full_width).astype(jnp.float32)
    summed = lax.psum_scatter(
        grouped.astype(jnp.bfloat16), "replica", scatter_dimension=0, tiled=True
    ).astype(jnp.float32)
    return summed.reshape(1, 1, slab_rows, full_width)


def update_block(summed, params, momentum):
    average = summed / lax.axis_size("replica")
    momentum_new = nesterov_keep * momentum + average
    params_new = params - outer_rate * (average + nesterov_keep * momentum_new)
    return (params_new, momentum_new, params_new.astype(jnp.bfloat16))


def spread_block(rounded):
    return lax.all_gather(rounded[0, 0], "replica", axis=0, tiled=True)


def local(enc_delta, enc_params, enc_momentum, dec_delta, dec_params, dec_momentum):
    results = []
    for deltas, params, momentum in (
        (enc_delta, enc_params, enc_momentum),
        (dec_delta, dec_params, dec_momentum),
    ):
        summed = reduce_block(deltas)
        params_new, momentum_new, rounded = update_block(summed, params, momentum)
        working = spread_block(rounded)
        results.append((params_new, momentum_new, working))
    return (
        results[0][0],
        results[0][1],
        results[0][2],
        results[1][0],
        results[1][1],
        results[1][2],
    )


def solution(mesh):
    return jax.shard_map(
        local,
        mesh=mesh,
        in_specs=(
            P("replica", "shard", None),
            P("replica", "shard", None, None),
            P("replica", "shard", None, None),
            P("replica", "shard", None),
            P("replica", "shard", None, None),
            P("replica", "shard", None, None),
        ),
        out_specs=(
            P("replica", "shard", None, None),
            P("replica", "shard", None, None),
            P("shard", None),
            P("replica", "shard", None, None),
            P("replica", "shard", None, None),
            P("shard", None),
        ),
        check_vma=False,
    )
```

profile of v0, /device:TPU:0, one launch (start us, length us, event | category | flops | bytes accessed | tf_op | source)
XLA Modules:
  0.0 354.5 jit_solution(9391848375553304368)
XLA Ops:
  7.2 0.0 reduce-scatter.5.cloned.1.call-start
  7.2 0.7 reduce-scatter.5.cloned.1.call-update
  7.9 0.0 reduce-scatter.3.cloned.1.call-start
  7.9 0.7 reduce-scatter.3.cloned.1.call-update
  8.6 0.0 all-gather.7.cloned.1.call-start
  8.7 89.0 %reduce-scatter.5.cloned.1.call-done = bf16[1,160,8192]{2,1,0:T(8,128)(2,1)} async-done(((bf16[4,160,8192]{2,1,0:T(8,128)(2,1)}), bf16[1,160,8192]{2,1,0:T(8,128)(2,1)}) %reduce-scatter.5.cloned.1.call-update) | async-done | bytes 2621456 | tf_op jit(solution)/shard_map/reduce_scatter | solution.py:16
  97.7 14.2 %fusion.4 = (bf16[1,1,160,8192]{3,2,1,0:T(8,128)(2,1)}, f32[1,1,160,8192]{3,2,1,0:T(8,128)}, f32[1,1,160,8192]{3,2,1,0:T(8,128)}) fusion(f32[1,1,160,8192]{3,2,1,0:T(8,128)} %param.10, bf16[1,160,8192]{2,1,0:T(8,128)(2,1)} %reduce-scatter.5.cloned.1.call-done, f32[1,1,160,8192]{3,2,1,0:T(8,128)} %param.11), kind=kLoop, calls=%fused_computation.10 | loop fusion | flops 11796480 | bytes 26214400 | tf_op jit(solution)/shard_map/convert_element_type | solution.py:26
  112.0 0.0 all-gather.7.cloned.1.call-update
  112.0 0.0 all-gather.5.cloned.1.call-start
  112.1 72.7 %reduce-scatter.3.cloned.1.call-done = bf16[1,160,8192]{2,1,0:T(8,128)(2,1)} async-done(((bf16[4,160,8192]{2,1,0:T(8,128)(2,1)}), bf16[1,160,8192]{2,1,0:T(8,128)(2,1)}) %reduce-scatter.3.cloned.1.call-update) | async-done | bytes 2621456 | tf_op jit(solution)/shard_map/reduce_scatter | solution.py:16
  184.8 13.1 %fusion.6 = (bf16[1,1,160,8192]{3,2,1,0:T(8,128)(2,1)}, f32[1,1,160,8192]{3,2,1,0:T(8,128)}, f32[1,1,160,8192]{3,2,1,0:T(8,128)}) fusion(f32[1,1,160,8192]{3,2,1,0:T(8,128)} %param.7, bf16[1,160,8192]{2,1,0:T(8,128)(2,1)} %reduce-scatter.3.cloned.1.call-done, f32[1,1,160,8192]{3,2,1,0:T(8,128)} %param.8), kind=kLoop, calls=%fused_computation.11 | loop fusion | flops 11796480 | bytes 26214400 | tf_op jit(solution)/shard_map/convert_element_type | solution.py:26
  197.9 0.0 all-gather.5.cloned.1.call-update
  197.9 59.2 %all-gather.7.cloned.1.call-done = bf16[1,1,640,8192]{3,2,1,0:T(8,128)(2,1)} async-done(((bf16[1,1,160,8192]{3,2,1,0:T(8,128)(2,1)}), bf16[1,1,640,8192]{3,2,1,0:T(8,128)(2,1)}) %all-gather.7.cloned.1.call-update) | async-done | bytes 10485776 | tf_op jit(solution)/shard_map/all_gather | solution.py:30
  257.1 72.2 %all-gather.5.cloned.1.call-done = bf16[1,1,640,8192]{3,2,1,0:T(8,128)(2,1)} async-done(((bf16[1,1,160,8192]{3,2,1,0:T(8,128)(2,1)}), bf16[1,1,640,8192]{3,2,1,0:T(8,128)(2,1)}) %all-gather.5.cloned.1.call-update) | async-done | bytes 10485776 | tf_op jit(solution)/shard_map/all_gather | solution.py:30
  329.3 9.3 %copy.14 = bf16[640,8192]{1,0:T(8,128)(2,1)} copy(bf16[640,8192]{1,0:T(8,128)(2,1)} %bitcast.25) | data formatting | bytes 20971520
  338.7 9.3 %copy.15 = bf16[640,8192]{1,0:T(8,128)(2,1)} copy(bf16[640,8192]{1,0:T(8,128)(2,1)} %bitcast.24) | data formatting | bytes 20971520
Async XLA Ops:
  7.2 90.6 %reduce-scatter.5.cloned.1.call-start = ((), (), s32[]{:S(2)}) async-start(), calls=%async_computation.3 | async-start | bytes 13107200 | tf_op jit(solution)/shard_map/reduce_scatter | solution.py:16
  7.9 176.9 %reduce-scatter.3.cloned.1.call-start = ((), (), s32[]{:S(2)}) async-start(), calls=%async_computation.2 | async-start | bytes 13107200 | tf_op jit(solution)/shard_map/reduce_scatter | solution.py:16
  8.6 248.5 %all-gather.7.cloned.1.call-start = ((), (), s32[]{:S(2)}) async-start(), calls=%async_computation.5 | async-start | bytes 13107200 | tf_op jit(solution)/shard_map/all_gather | solution.py:30
  112.0 217.3 %all-gather.5.cloned.1.call-start = ((), (), s32[]{:S(2)}) async-start(), calls=%async_computation.4 | async-start | bytes 13107200 | tf_op jit(solution)/shard_map/all_gather | solution.py:30
Sparse Core Ops, SparseCore 0:
  10.6 87.1 reduce-scatter.4
  100.3 84.4 reduce-scatter.2
  186.9 70.1 all-gather.6
  259.1 70.1 all-gather.4
where the time goes:
time: 355 us
  waiting for transfers between devices  295 us (83%)
  other arithmetic  27.3 us (8%)
  local copies, waits for them, and re-layouts  18.7 us (5%)
  between operations  13.8 us (4%)
    reduce_scatter x2, waiting for transfers between devices, reduce_block(): lax.psum_scatter(grouped.astype(jnp.bfloat16), 'replica', scatter_dimensi...  162 us
    all_gather x2, waiting for transfers between devices, spread_block(): return lax.all_gather(rounded[0, 0], 'replica', axis=0, tiled=True)  131 us
    convert_element_type x2, other arithmetic, update_block(): return (params_new, momentum_new, params_new.astype(jnp.bfloat16))  27.3 us
    unnamed x2, local copies, waits for them, and re-layouts  18.7 us
  transfers between devices with their start and end apart: 4, of which 4 were waited for; matrix products, arithmetic and copies ran while one was open for 8% of the time, Pallas kernels for 0%

commit v1 on v0

v1 whole, which is shorter than its diff:
```python
import functools

import jax
import jax.numpy as jnp
from jax import lax
from jax.experimental import pallas as pl
from jax.experimental.pallas import tpu as pltpu
from jax.sharding import PartitionSpec as P


outer_rate = 0.7
nesterov_keep = 0.9
lane = 128
widest = 8
vmem_bytes = 67_043_328

first_shares = (4, 4, 8, 16, 32)
last_shares = (32, 16, 8, 4, 4)

f32 = jnp.float32
bf16 = jnp.bfloat16


def chunks_of(columns, shares):
    units = columns // lane
    total = sum(shares)
    edges, seen = [0], 0
    for share in shares:
        seen += share
        edges.append(max(edges[-1], units * seen // total))
    return [(a, b - a) for a, b in zip(edges[:-1], edges[1:]) if b > a]


def step_of(start, width):
    for units in (widest, 4, 2, 1):
        if start % units == 0 and width % units == 0:
            return units
    return 1


def me():
    return lax.axis_index("replica")


def near_of(r):
    return r + 1 - 2 * lax.rem(r, 2)


def far_of(r):
    half = lax.axis_size("replica") // 2
    return lax.rem(r + half, 2 * half)


def slab_spec(rows, step, start, which):
    return pl.BlockSpec(
        (1, rows, step * lane),
        lambda i: (which(me()), 0, start // step + i),
    )


def state_spec(rows, step, start):
    return pl.BlockSpec((rows, step * lane), lambda i: (0, start // step + i))


def pair_spec(rows, step):
    return pl.BlockSpec((2, rows, step * lane), lambda i: (0, 0, i))


def same(r):
    return r


def near_far(r):
    return far_of(near_of(r))


def estimate(bytes_moved):
    return pl.CostEstimate(
        flops=bytes_moved, bytes_accessed=bytes_moved, transcendentals=0
    )


def compiler_params():
    return pltpu.CompilerParams(vmem_limit_bytes=vmem_bytes)


def pick_kernel(one_ref, two_ref, *refs):
    out_ref = refs[-1]
    out_ref[0] = one_ref[0]
    out_ref[1] = two_ref[0]


def pick(delta, start, width, after):
    _, rows, _ = delta.shape
    step = step_of(start, width)
    return pl.pallas_call(
        pick_kernel,
        grid=(width // step,),
        in_specs=[
            slab_spec(rows, step, start, near_of),
            slab_spec(rows, step, start, near_far),
        ]
        + [pl.BlockSpec(memory_space=pl.ANY)] * len(after),
        out_specs=pair_spec(rows, step),
        out_shape=pltpu.HBM((2, rows, width * lane), bf16),
        cost_estimate=estimate(8 * rows * width * lane),
        compiler_params=compiler_params(),
        name="pick",
    )(delta, delta, *after)


def share(replicas):
    return outer_rate * (1 + nesterov_keep) / replicas


def send_kernel(
    replicas, own_ref, away_ref, got_ref, params_ref, momentum_ref, out_ref
):
    out_ref[0] = (away_ref[0].astype(f32) + got_ref[1].astype(f32)).astype(bf16)
    summed = own_ref[0].astype(f32) + got_ref[0].astype(f32)
    base = params_ref[...] - (outer_rate * nesterov_keep**2) * momentum_ref[...]
    out_ref[1] = (base - share(replicas) * summed).astype(bf16)


def send_part(replicas, delta, got, params, momentum, start, width):
    _, rows, _ = delta.shape
    step = step_of(start, width)
    return pl.pallas_call(
        functools.partial(send_kernel, replicas),
        grid=(width // step,),
        in_specs=[
            slab_spec(rows, step, start, same),
            slab_spec(rows, step, start, far_of),
            pair_spec(rows, step),
            state_spec(rows, step, start),
            state_spec(rows, step, start),
        ],
        out_specs=pair_spec(rows, step),
        out_shape=pltpu.HBM((2, rows, width * lane), bf16),
        cost_estimate=estimate(20 * rows * width * lane),
        compiler_params=compiler_params(),
        name="send_part",
    )(delta, delta, got, params, momentum)


def finish_kernel(
    replicas,
    own_ref,
    got_ref,
    sent_ref,
    far_ref,
    near_sent_ref,
    near_far_ref,
    params_ref,
    momentum_ref,
    *refs,
):
    params_new_ref, momentum_new_ref, working_ref = refs[-3:]
    r = me()
    k = share(replicas)

    def joined(base, summed):
        return (base.astype(f32) - k * summed.astype(f32)).astype(bf16)

    summed = own_ref[0].astype(f32) + got_ref[0].astype(f32)
    average = (summed + far_ref[0].astype(f32)) * (1 / replicas)
    momentum_new = nesterov_keep * momentum_ref[...] + average
    momentum_new_ref[...] = momentum_new
    params_new_ref[...] = params_ref[...] - outer_rate * (
        average + nesterov_keep * momentum_new
    )
    working_ref[r] = joined(sent_ref[1], far_ref[0])
    working_ref[far_of(r)] = joined(far_ref[1], sent_ref[0])
    working_ref[near_of(r)] = joined(near_sent_ref[1], near_far_ref[0])
    working_ref[near_far(r)] = joined(near_far_ref[1], near_sent_ref[0])


def finish(
    replicas, delta, got, sent, far, near_sent, near_far_got, params, momentum,
    start, width, results, after,
):
    _, rows, columns = delta.shape
    step = step_of(start, width)
    out_shape = (
        jax.ShapeDtypeStruct((rows, columns), f32),
        jax.ShapeDtypeStruct((rows, columns), f32),
        jax.ShapeDtypeStruct((replicas, rows, columns), bf16),
    )
    operands = [delta, got, sent, far, near_sent, near_far_got, params, momentum]
    pair = pair_spec(rows, step)
    in_specs = [
        slab_spec(rows, step, start, same), pair, pair, pair, pair, pair,
        state_spec(rows, step, start), state_spec(rows, step, start),
    ]
    aliases = {}
    for array in after:
        operands.append(array)
        in_specs.append(pl.BlockSpec(memory_space=pl.ANY))
    if results is not None:
        for i, array in enumerate(results):
            aliases[len(operands)] = i
            operands.append(array)
            in_specs.append(pl.BlockSpec(memory_space=pl.ANY))
    return pl.pallas_call(
        functools.partial(finish_kernel, replicas),
        grid=(width // step,),
        in_specs=in_specs,
        out_specs=(
            state_spec(rows, step, start),
            state_spec(rows, step, start),
            pl.BlockSpec(
                (replicas, rows, step * lane), lambda i: (0, 0, start // step + i)
            ),
        ),
        out_shape=out_shape,
        input_output_aliases=aliases,
        cost_estimate=estimate(44 * rows * width * lane),
        compiler_params=compiler_params(),
        name="finish",
    )(*operands)


def local(enc_delta, enc_params, enc_momentum, dec_delta, dec_params, dec_momentum):
    replicas = lax.axis_size("replica")
    near = [(r, r + 1 - 2 * (r % 2)) for r in range(replicas)]
    far = [(r, (r + replicas // 2) % replicas) for r in range(replicas)]

    def swap(x, pairs):
        return lax.ppermute(x, "replica", pairs)

    parts = []
    for block, (deltas, params, momentum, shares) in enumerate((
        (enc_delta, enc_params, enc_momentum, first_shares),
        (dec_delta, dec_params, dec_momentum, last_shares),
    )):
        _, _, rows, columns = params.shape
        delta = deltas.reshape(replicas, rows, columns)
        params = params.reshape(rows, columns)
        momentum = momentum.reshape(rows, columns)
        for start, width in chunks_of(columns, shares):
            parts.append((block, delta, params, momentum, start, width))

    gots, sents, cames, near_sents = [], [], [], []
    for i, (_, delta, params, momentum, start, width) in enumerate(parts):
        picked = pick(delta, start, width, sents[i - 2 : i - 1] if i > 1 else [])
        got = swap(picked, near)
        sent = send_part(replicas, delta, got, params, momentum, start, width)
        came = swap(sent, far)
        near_sent = swap(sent, near)
        gots.append(got)
        sents.append(sent)
        cames.append(came)
        near_sents.append(near_sent)

    arrays = [None, None]
    after = sents[-1:]
    for i, (block, delta, params, momentum, start, width) in enumerate(parts):
        near_came = swap(cames[i], near)
        arrays[block] = finish(
            replicas, delta, gots[i], sents[i], cames[i], near_sents[i], near_came,
            params, momentum, start, width, arrays[block], after,
        )
        after = []

    results = []
    for params_new, momentum_new, working in arrays:
        rows, columns = params_new.shape
        results.append(
            (
                params_new.reshape(1, 1, rows, columns),
                momentum_new.reshape(1, 1, rows, columns),
                working.reshape(replicas * rows, columns),
            )
        )
    return (*results[0], *results[1])


def solution(mesh):
    delta_spec = P("replica", "shard", None)
    state = P("replica", "shard", None, None)
    return jax.shard_map(
        local,
        mesh=mesh,
        in_specs=(delta_spec, state, state, delta_spec, state, state),
        out_specs=(state, state, P("shard", None), state, state, P("shard", None)),
        check_vma=False,
    )
```

time: 355 us -> 344 us (0.969)
  Pallas kernels: 0 us -> 110 us
  waiting for transfers between devices: 295 us -> 213 us
  other arithmetic: 27.3 us -> 0 us
  starting transfers between devices: 0.16 us -> 20.4 us
  local copies, waits for them, and re-layouts: 18.7 us -> 0 us
  between operations: 13.8 us -> 0.7 us
    ppermute x0 -> x40, waiting for transfers between devices: none -> 213 us  [swap(): return lax.ppermute(x, 'replica', pairs)]
    reduce_scatter x2 -> x0, waiting for transfers between devices: 162 us -> none  [reduce_block(): lax.psum_scatter(grouped.astype(jnp.bfloat16), 'replica', scatter_dimensi...]
    all_gather x2 -> x0, waiting for transfers between devices: 131 us -> none  [spread_block(): return lax.all_gather(rounded[0, 0], 'replica', axis=0, tiled=True)]
    pallas_call x0 -> x30, Pallas kernels: none -> 110 us  [the longest x10 53.2 us: finish(): pl.pallas_call(functools.partial(finish_kernel, replicas), grid=(width //...]
    convert_element_type x2 -> x0, other arithmetic: 27.3 us -> none  [update_block(): return (params_new, momentum_new, params_new.astype(jnp.bfloat16))]
    ppermute x0 -> x40, starting transfers between devices: none -> 20.4 us  [swap(): return lax.ppermute(x, 'replica', pairs)]
    unnamed x2 -> x0, local copies, waits for them, and re-layouts: 18.7 us -> none
  transfers between devices with their start and end apart: 4 -> 40, of which waited for: 4 -> 11; matrix products, arithmetic and copies ran while one was open for 8% -> 0% of each run, Pallas kernels for 0% -> 29%
where the time goes in v1:
time: 344 us
  waiting for transfers between devices  213 us (62%)
  Pallas kernels  110 us (32%)
  starting transfers between devices  20.4 us (6%)
    ppermute x40, waiting for transfers between devices, swap(): return lax.ppermute(x, 'replica', pairs)  213 us
    pallas_call x10, Pallas kernels, finish(): pl.pallas_call(functools.partial(finish_kernel, replicas), grid=(width //...  53.2 us
    pallas_call x10, Pallas kernels, send_part(): pl.pallas_call(functools.partial(send_kernel, replicas), grid=(width // s...  33.5 us
    pallas_call x10, Pallas kernels, pick(): pl.pallas_call(pick_kernel, grid=(width // step,), in_specs=[slab_spec(ro...  23.1 us
    ppermute x40, starting transfers between devices, swap(): return lax.ppermute(x, 'replica', pairs)  20.4 us
  transfers between devices with their start and end apart: 40, of which 11 were waited for; matrix products, arithmetic and copies ran while one was open for 0% of the time, Pallas kernels for 29%

profile of v1, /device:TPU:0, one launch (start us, length us, event | category | flops | bytes accessed | tf_op | source)
XLA Modules:
  0.0 343.7 jit_solution(16783547243010787253)
XLA Ops:
  19.9 4.0 %pick.12 = bf16[2,160,4096]{2,1,0:T(8,128)(2,1)} custom-call(bf16[4,160,8192]{2,1,0:T(8,128)(2,1)} %bitcast.26, bf16[4,160,8192]{2,1,0:T(8,128)(2,1)} %bitcast.27, bf16[2,160,1024]{2,1,0:T(8,128)(2,1)} %send_part.11.refs_0_.sent_ref), custom_call_target="tpu_custom_call" | custom-call | flops 5242880 | bytes 5242880 | tf_op jit(solution)/shard_map/pick/pallas_call | solution.py:96
  24.2 3.6 %send_part.14.refs_0_.sent_ref = bf16[2,160,2048]{2,1,0:T(8,128)(2,1)} custom-call(bf16[4,160,8192]{2,1,0:T(8,128)(2,1)} %bitcast.28, bf16[4,160,8192]{2,1,0:T(8,128)(2,1)} %bitcast.29, bf16[2,160,2048]{2,1,0:T(8,128)(2,1)} %collective-permute-done.7.got_ref, f32[160,8192]{1,0:T(8,128)} %bitcast.65, f32[160,8192]{1,0:T(8,128)} %bitcast.75), custom_call_target="tpu_custom_call" | custom-call | flops 6553600 | bytes 6553600 | tf_op jit(solution)/shard_map/send_part/pallas_call | solution.py:128
  27.8 4.0 %pick.15 = bf16[2,160,4096]{2,1,0:T(8,128)(2,1)} custom-call(bf16[4,160,8192]{2,1,0:T(8,128)(2,1)} %bitcast.37, bf16[4,160,8192]{2,1,0:T(8,128)(2,1)} %bitcast.38, bf16[2,160,2048]{2,1,0:T(8,128)(2,1)} %send_part.14.refs_0_.sent_ref), custom_call_target="tpu_custom_call" | custom-call | flops 5242880 | bytes 5242880 | tf_op jit(solution)/shard_map/pick/pallas_call | solution.py:96
  31.9 2.9 collective-permute-start.17
  34.9 8.7 %collective-permute-done.17.far_ref = bf16[2,160,512]{2,1,0:T(8,128)(2,1)} collective-permute-done((bf16[2,160,512]{2,1,0:T(8,128)(2,1)}, bf16[2,160,512]{2,1,0:T(8,128)(2,1)}, u32[]{:S(2)}, u32[]{:S(2)}) %collective-permute-start.17) | collective-permute-done | bytes 327712 | tf_op jit(solution)/shard_map/ppermute | solution.py:229
  45.6 5.0 %collective-permute-done.14.far_ref = bf16[2,160,512]{2,1,0:T(8,128)(2,1)} collective-permute-done((bf16[2,160,512]{2,1,0:T(8,128)(2,1)}, bf16[2,160,512]{2,1,0:T(8,128)(2,1)}, u32[]{:S(2)}, u32[]{:S(2)}) %collective-permute-start.14) | collective-permute-done | bytes 327712 | tf_op jit(solution)/shard_map/ppermute | solution.py:229
  52.7 6.1 %send_part.12.sent_ref.refs_0_ = bf16[2,160,4096]{2,1,0:T(8,128)(2,1)} custom-call(bf16[4,160,8192]{2,1,0:T(8,128)(2,1)} %bitcast.30, bf16[4,160,8192]{2,1,0:T(8,128)(2,1)} %bitcast.31, bf16[2,160,4096]{2,1,0:T(8,128)(2,1)} %collective-permute-done.2.got_ref, f32[160,8192]{1,0:T(8,128)} %bitcast.66, f32[160,8192]{1,0:T(8,128)} %bitcast.76), custom_call_target="tpu_custom_call" | custom-call | flops 13107200 | bytes 13107200 | tf_op jit(solution)/shard_map/send_part/pallas_call | solution.py:128
  61.4 3.3 collective-permute-done.16.near_far_ref
  65.0 27.2 %collective-permute-done.11.far_ref = bf16[2,160,1024]{2,1,0:T(8,128)(2,1)} collective-permute-done((bf16[2,160,1024]{2,1,0:T(8,128)(2,1)}, bf16[2,160,1024]{2,1,0:T(8,128)(2,1)}, u32[]{:S(2)}, u32[]{:S(2)}) %collective-permute-start.11) | collective-permute-done | bytes 655392 | tf_op jit(solution)/shard_map/ppermute | solution.py:229
  92.8 6.1 %send_part.15.refs_0_.sent_ref = bf16[2,160,4096]{2,1,0:T(8,128)(2,1)} custom-call(bf16[4,160,8192]{2,1,0:T(8,128)(2,1)} %bitcast.41, bf16[4,160,8192]{2,1,0:T(8,128)(2,1)} %bitcast.42, bf16[2,160,4096]{2,1,0:T(8,128)(2,1)} %collective-permute-done.20.got_ref, f32[160,8192]{1,0:T(8,128)} %bitcast.82, f32[160,8192]{1,0:T(8,128)} %bitcast.92), custom_call_target="tpu_custom_call" | custom-call | flops 13107200 | bytes 13107200 | tf_op jit(solution)/shard_map/send_part/pallas_call | solution.py:128
  102.9 3.6 %send_part.18.refs_0_.sent_ref = bf16[2,160,2048]{2,1,0:T(8,128)(2,1)} custom-call(bf16[4,160,8192]{2,1,0:T(8,128)(2,1)} %bitcast.45, bf16[4,160,8192]{2,1,0:T(8,128)(2,1)} %bitcast.46, bf16[2,160,2048]{2,1,0:T(8,128)(2,1)} %collective-permute-done.26.got_ref, f32[160,8192]{1,0:T(8,128)} %bitcast.83, f32[160,8192]{1,0:T(8,128)} %bitcast.93), custom_call_target="tpu_custom_call" | custom-call | flops 6553600 | bytes 6553600 | tf_op jit(solution)/shard_map/send_part/pallas_call | solution.py:128
  117.5 111.7 %collective-permute-done.31.far_ref = bf16[2,160,1024]{2,1,0:T(8,128)(2,1)} collective-permute-done((bf16[2,160,1024]{2,1,0:T(8,128)(2,1)}, bf16[2,160,1024]{2,1,0:T(8,128)(2,1)}, u32[]{:S(2)}, u32[]{:S(2)}) %collective-permute-start.31) | collective-permute-done | bytes 655392 | tf_op jit(solution)/shard_map/ppermute | solution.py:229
  233.1 30.6 %collective-permute-done.28.far_ref = bf16[2,160,512]{2,1,0:T(8,128)(2,1)} collective-permute-done((bf16[2,160,512]{2,1,0:T(8,128)(2,1)}, bf16[2,160,512]{2,1,0:T(8,128)(2,1)}, u32[]{:S(2)}, u32[]{:S(2)}) %collective-permute-start.28) | collective-permute-done | bytes 327712 | tf_op jit(solution)/shard_map/ppermute | solution.py:229
  265.5 7.8 %collective-permute-done.23.far_ref = bf16[2,160,512]{2,1,0:T(8,128)(2,1)} collective-permute-done((bf16[2,160,512]{2,1,0:T(8,128)(2,1)}, bf16[2,160,512]{2,1,0:T(8,128)(2,1)}, u32[]{:S(2)}, u32[]{:S(2)}) %collective-permute-start.23) | collective-permute-done | bytes 327712 | tf_op jit(solution)/shard_map/ppermute | solution.py:229
  274.3 6.1 %collective-permute-done.35.near_sent_ref = bf16[2,160,2048]{2,1,0:T(8,128)(2,1)} collective-permute-done((bf16[2,160,2048]{2,1,0:T(8,128)(2,1)}, bf16[2,160,2048]{2,1,0:T(8,128)(2,1)}, u32[]{:S(2)}, u32[]{:S(2)}) %collective-permute-start.35) | collective-permute-done | bytes 1310752 | tf_op jit(solution)/shard_map/ppermute | solution.py:229
  281.1 8.7 %collective-permute-done.36.near_far_ref = bf16[2,160,2048]{2,1,0:T(8,128)(2,1)} collective-permute-done((bf16[2,160,2048]{2,1,0:T(8,128)(2,1)}, bf16[2,160,2048]{2,1,0:T(8,128)(2,1)}, u32[]{:S(2)}, u32[]{:S(2)}) %collective-permute-start.36) | collective-permute-done | bytes 1310752 | tf_op jit(solution)/shard_map/ppermute | solution.py:229
  296.2 4.2 %finish.12 = (f32[160,8192]{1,0:T(8,128)}, f32[160,8192]{1,0:T(8,128)}, bf16[4,160,8192]{2,1,0:T(8,128)(2,1)}) custom-call(bf16[4,160,8192]{2,1,0:T(8,128)(2,1)} %bitcast.34, bf16[2,160,1024]{2,1,0:T(8,128)(2,1)} %collective-permute-done.1.got_ref, ...), custom_call_target="tpu_custom_call", output_to_operand_aliasing={{0}: (8, {}), {1}: (9, {}), {2}: (10, {})} | custom-call | flops 7208960 | bytes 7208960 | tf_op jit(solution)/shard_map/finish/pallas_call | solution.py:204
  300.4 5.9 %finish.13 = (f32[160,8192]{1,0:T(8,128)}, f32[160,8192]{1,0:T(8,128)}, bf16[4,160,8192]{2,1,0:T(8,128)(2,1)}) custom-call(bf16[4,160,8192]{2,1,0:T(8,128)(2,1)} %bitcast.35, bf16[2,160,2048]{2,1,0:T(8,128)(2,1)} %collective-permute-done.7.got_ref, ...), custom_call_target="tpu_custom_call", output_to_operand_aliasing={{0}: (8, {}), {1}: (9, {}), {2}: (10, {})} | custom-call | flops 14417920 | bytes 14417920 | tf_op jit(solution)/shard_map/finish/pallas_call | solution.py:204
  306.3 10.8 %finish.14 = (f32[160,8192]{1,0:T(8,128)}, f32[160,8192]{1,0:T(8,128)}, bf16[4,160,8192]{2,1,0:T(8,128)(2,1)}) custom-call(bf16[4,160,8192]{2,1,0:T(8,128)(2,1)} %bitcast.36, bf16[2,160,4096]{2,1,0:T(8,128)(2,1)} %collective-permute-done.2.got_ref, ...), custom_call_target="tpu_custom_call", output_to_operand_aliasing={{0}: (8, {}), {1}: (9, {}), {2}: (10, {})} | custom-call | flops 28835840 | bytes 28835840 | tf_op jit(solution)/shard_map/finish/pallas_call | solution.py:204
  317.2 10.6 %finish.15 = (f32[160,8192]{1,0:T(8,128)}, f32[160,8192]{1,0:T(8,128)}, bf16[4,160,8192]{2,1,0:T(8,128)(2,1)}) custom-call(bf16[4,160,8192]{2,1,0:T(8,128)(2,1)} %bitcast.57, bf16[2,160,4096]{2,1,0:T(8,128)(2,1)} %collective-permute-done.20.got_ref, bf16[2,160,4096]{2,1,0:T(8,128)(2,1)} %send_part.15.refs_0_.sent_ref, ...), custom_call_target="tpu_custom_call" | custom-call | flops 28835840 | bytes 28835840 | tf_op jit(solution)/shard_map/finish/pallas_call | solution.py:204
  327.8 5.9 %finish.16 = (f32[160,8192]{1,0:T(8,128)}, f32[160,8192]{1,0:T(8,128)}, bf16[4,160,8192]{2,1,0:T(8,128)(2,1)}) custom-call(bf16[4,160,8192]{2,1,0:T(8,128)(2,1)} %bitcast.58, bf16[2,160,2048]{2,1,0:T(8,128)(2,1)} %collective-permute-done.26.got_ref, ...), custom_call_target="tpu_custom_call", output_to_operand_aliasing={{0}: (8, {}), {1}: (9, {}), {2}: (10, {})} | custom-call | flops 14417920 | bytes 14417920 | tf_op jit(solution)/shard_map/finish/pallas_call | solution.py:204
  333.7 4.2 %finish.17 = (f32[160,8192]{1,0:T(8,128)}, f32[160,8192]{1,0:T(8,128)}, bf16[4,160,8192]{2,1,0:T(8,128)(2,1)}) custom-call(bf16[4,160,8192]{2,1,0:T(8,128)(2,1)} %bitcast.59, bf16[2,160,1024]{2,1,0:T(8,128)(2,1)} %collective-permute-done.21.got_ref, ...), custom_call_target="tpu_custom_call", output_to_operand_aliasing={{0}: (8, {}), {1}: (9, {}), {2}: (10, {})} | custom-call | flops 7208960 | bytes 7208960 | tf_op jit(solution)/shard_map/finish/pallas_call | solution.py:204
  337.9 2.9 finish.18
  340.8 2.9 finish.19
  (86 shorter events, 56.1 us)
Async XLA Ops:
  23.8 26.8 %collective-permute-start.2 = (bf16[2,160,4096]{2,1,0:T(8,128)(2,1)}, bf16[2,160,4096]{2,1,0:T(8,128)(2,1)}, u32[]{:S(2)}, u32[]{:S(2)}) collective-permute-start(bf16[2,160,4096]{2,1,0:T(8,128)(2,1)} %pick.12), channel_id=1, source_target_pairs={{0,8},{8,0},{16,24},{24,16},{1,9},{9,1},{17,25},{25,17},{2,10},{10... | collective-permute-start | bytes 7864328 | tf_op jit(solution)/shard_map/ppermute | solution.py:229
  31.7 61.0 %collective-permute-start.20 = (bf16[2,160,4096]{2,1,0:T(8,128)(2,1)}, bf16[2,160,4096]{2,1,0:T(8,128)(2,1)}, u32[]{:S(2)}, u32[]{:S(2)}) collective-permute-start(bf16[2,160,4096]{2,1,0:T(8,128)(2,1)} %pick.15), channel_id=1, source_target_pairs={{0,8},{8,0},{16,24},{24,16},{1,9},{9,1},{17,25},{25,17},{2,10},{10... | collective-permute-start | bytes 7864328 | tf_op jit(solution)/shard_map/ppermute | solution.py:229
  34.7 15.9 %collective-permute-start.14 = (bf16[2,160,512]{2,1,0:T(8,128)(2,1)}, bf16[2,160,512]{2,1,0:T(8,128)(2,1)}, u32[]{:S(2)}, u32[]{:S(2)}) collective-permute-start(bf16[2,160,512]{2,1,0:T(8,128)(2,1)} %send_part.13.refs_0_.sent_ref), channel_id=1, source_target_pairs={{0,16},{8,24},{16,0},{24,8},{1,17},{9,25},{17,1},{25,9},{2,18},{10... | collective-permute-start | bytes 983048 | tf_op jit(solution)/shard_map/ppermute | solution.py:229
  43.6 48.6 %collective-permute-start.8 = (bf16[2,160,2048]{2,1,0:T(8,128)(2,1)}, bf16[2,160,2048]{2,1,0:T(8,128)(2,1)}, u32[]{:S(2)}, u32[]{:S(2)}) collective-permute-start(bf16[2,160,2048]{2,1,0:T(8,128)(2,1)} %send_part.14.refs_0_.sent_ref), channel_id=1, source_target_pairs={{0,16},{8,24},{16,0},{24,8},{1,17},{9,25},{17,1},{25,9},{2,18},{10... | collective-permute-start | bytes 3932168 | tf_op jit(solution)/shard_map/ppermute | solution.py:229
  45.6 15.3 %collective-permute-start.15 = (bf16[2,160,512]{2,1,0:T(8,128)(2,1)}, bf16[2,160,512]{2,1,0:T(8,128)(2,1)}, u32[]{:S(2)}, u32[]{:S(2)}) collective-permute-start(bf16[2,160,512]{2,1,0:T(8,128)(2,1)} %send_part.13.refs_0_.sent_ref), channel_id=1, source_target_pairs={{0,8},{8,0},{16,24},{24,16},{1,9},{9,1},{17,25},{25,17},{2,10},{10... | collective-permute-start | bytes 983048 | tf_op jit(solution)/shard_map/ppermute | solution.py:229
  50.6 41.6 %collective-permute-start.11 = (bf16[2,160,1024]{2,1,0:T(8,128)(2,1)}, bf16[2,160,1024]{2,1,0:T(8,128)(2,1)}, u32[]{:S(2)}, u32[]{:S(2)}) collective-permute-start(bf16[2,160,1024]{2,1,0:T(8,128)(2,1)} %send_part.11.refs_0_.sent_ref), channel_id=1, source_target_pairs={{0,16},{8,24},{16,0},{24,8},{1,17},{9,25},{17,1},{25,9},{2,18},{10... | collective-permute-start | bytes 1966088 | tf_op jit(solution)/shard_map/ppermute | solution.py:229
  60.9 42.0 %collective-permute-start.26 = (bf16[2,160,2048]{2,1,0:T(8,128)(2,1)}, bf16[2,160,2048]{2,1,0:T(8,128)(2,1)}, u32[]{:S(2)}, u32[]{:S(2)}) collective-permute-start(bf16[2,160,2048]{2,1,0:T(8,128)(2,1)} %pick.18), channel_id=1, source_target_pairs={{0,8},{8,0},{16,24},{24,16},{1,9},{9,1},{17,25},{25,17},{2,10},{10... | collective-permute-start | bytes 3932168 | tf_op jit(solution)/shard_map/ppermute | solution.py:229
  64.8 34.2 %collective-permute-start.12 = (bf16[2,160,1024]{2,1,0:T(8,128)(2,1)}, bf16[2,160,1024]{2,1,0:T(8,128)(2,1)}, u32[]{:S(2)}, u32[]{:S(2)}) collective-permute-start(bf16[2,160,1024]{2,1,0:T(8,128)(2,1)} %send_part.11.refs_0_.sent_ref), channel_id=1, source_target_pairs={{0,8},{8,0},{16,24},{24,16},{1,9},{9,1},{17,25},{25,17},{2,10},{10... | collective-permute-start | bytes 1966088 | tf_op jit(solution)/shard_map/ppermute | solution.py:229
  92.2 21.0 %collective-permute-start.9 = (bf16[2,160,2048]{2,1,0:T(8,128)(2,1)}, bf16[2,160,2048]{2,1,0:T(8,128)(2,1)}, u32[]{:S(2)}, u32[]{:S(2)}) collective-permute-start(bf16[2,160,2048]{2,1,0:T(8,128)(2,1)} %send_part.14.refs_0_.sent_ref), channel_id=1, source_target_pairs={{0,8},{8,0},{16,24},{24,16},{1,9},{9,1},{17,25},{25,17},{2,10},{10... | collective-permute-start | bytes 3932168 | tf_op jit(solution)/shard_map/ppermute | solution.py:229
  92.7 20.6 %collective-permute-start.10 = (bf16[2,160,2048]{2,1,0:T(8,128)(2,1)}, bf16[2,160,2048]{2,1,0:T(8,128)(2,1)}, u32[]{:S(2)}, u32[]{:S(2)}) collective-permute-start(bf16[2,160,2048]{2,1,0:T(8,128)(2,1)} %collective-permute-done.8.far_ref), channel_id=1, source_target_pairs={{0,8},{8,0},{16,24},{24,16},{1,9},{9,1},{17,25},{25,17},{2,10},{10... | collective-permute-start | bytes 3932168 | tf_op jit(solution)/shard_map/ppermute | solution.py:229
  98.9 174.9 %collective-permute-start.3 = (bf16[2,160,4096]{2,1,0:T(8,128)(2,1)}, bf16[2,160,4096]{2,1,0:T(8,128)(2,1)}, u32[]{:S(2)}, u32[]{:S(2)}) collective-permute-start(bf16[2,160,4096]{2,1,0:T(8,128)(2,1)} %send_part.12.sent_ref.refs_0_), channel_id=1, source_target_pairs={{0,16},{8,24},{16,0},{24,8},{1,17},{9,25},{17,1},{25,9},{2,18},{10... | collective-permute-start | bytes 7864328 | tf_op jit(solution)/shard_map/ppermute | solution.py:229
  100.7 173.2 %collective-permute-start.37 = (bf16[2,160,4096]{2,1,0:T(8,128)(2,1)}, bf16[2,160,4096]{2,1,0:T(8,128)(2,1)}, u32[]{:S(2)}, u32[]{:S(2)}) collective-permute-start(bf16[2,160,4096]{2,1,0:T(8,128)(2,1)} %send_part.15.refs_0_.sent_ref), channel_id=1, source_target_pairs={{0,16},{8,24},{16,0},{24,8},{1,17},{9,25},{17,1},{25,9},{2,18},{10... | collective-permute-start | bytes 7864328 | tf_op jit(solution)/shard_map/ppermute | solution.py:229
  113.3 115.9 %collective-permute-start.31 = (bf16[2,160,1024]{2,1,0:T(8,128)(2,1)}, bf16[2,160,1024]{2,1,0:T(8,128)(2,1)}, u32[]{:S(2)}, u32[]{:S(2)}) collective-permute-start(bf16[2,160,1024]{2,1,0:T(8,128)(2,1)} %send_part.16.refs_0_.sent_ref), channel_id=1, source_target_pairs={{0,16},{8,24},{16,0},{24,8},{1,17},{9,25},{17,1},{25,9},{2,18},{10... | collective-permute-start | bytes 1966088 | tf_op jit(solution)/shard_map/ppermute | solution.py:229
  115.1 158.2 %collective-permute-start.34 = (bf16[2,160,2048]{2,1,0:T(8,128)(2,1)}, bf16[2,160,2048]{2,1,0:T(8,128)(2,1)}, u32[]{:S(2)}, u32[]{:S(2)}) collective-permute-start(bf16[2,160,2048]{2,1,0:T(8,128)(2,1)} %send_part.18.refs_0_.sent_ref), channel_id=1, source_target_pairs={{0,16},{8,24},{16,0},{24,8},{1,17},{9,25},{17,1},{25,9},{2,18},{10... | collective-permute-start | bytes 3932168 | tf_op jit(solution)/shard_map/ppermute | solution.py:229
  115.4 115.6 %collective-permute-start.32 = (bf16[2,160,1024]{2,1,0:T(8,128)(2,1)}, bf16[2,160,1024]{2,1,0:T(8,128)(2,1)}, u32[]{:S(2)}, u32[]{:S(2)}) collective-permute-start(bf16[2,160,1024]{2,1,0:T(8,128)(2,1)} %send_part.16.refs_0_.sent_ref), channel_id=1, source_target_pairs={{0,8},{8,0},{16,24},{24,16},{1,9},{9,1},{17,25},{25,17},{2,10},{10... | collective-permute-start | bytes 1966088 | tf_op jit(solution)/shard_map/ppermute | solution.py:229
  229.2 34.6 %collective-permute-start.28 = (bf16[2,160,512]{2,1,0:T(8,128)(2,1)}, bf16[2,160,512]{2,1,0:T(8,128)(2,1)}, u32[]{:S(2)}, u32[]{:S(2)}) collective-permute-start(bf16[2,160,512]{2,1,0:T(8,128)(2,1)} %send_part.19.sent_ref), channel_id=1, source_target_pairs={{0,16},{8,24},{16,0},{24,8},{1,17},{9,25},{17,1},{25,9},{2,18},{10... | collective-permute-start | bytes 983048 | tf_op jit(solution)/shard_map/ppermute | solution.py:229
  231.0 49.6 %collective-permute-start.4 = (bf16[2,160,4096]{2,1,0:T(8,128)(2,1)}, bf16[2,160,4096]{2,1,0:T(8,128)(2,1)}, u32[]{:S(2)}, u32[]{:S(2)}) collective-permute-start(bf16[2,160,4096]{2,1,0:T(8,128)(2,1)} %send_part.12.sent_ref.refs_0_), channel_id=1, source_target_pairs={{0,8},{8,0},{16,24},{24,16},{1,9},{9,1},{17,25},{25,17},{2,10},{10... | collective-permute-start | bytes 7864328 | tf_op jit(solution)/shard_map/ppermute | solution.py:229
  273.8 16.1 %collective-permute-start.5 = (bf16[2,160,4096]{2,1,0:T(8,128)(2,1)}, bf16[2,160,4096]{2,1,0:T(8,128)(2,1)}, u32[]{:S(2)}, u32[]{:S(2)}) collective-permute-start(bf16[2,160,4096]{2,1,0:T(8,128)(2,1)} %collective-permute-done.3.far_ref), channel_id=1, source_target_pairs={{0,8},{8,0},{16,24},{24,16},{1,9},{9,1},{17,25},{25,17},{2,10},{10... | collective-permute-start | bytes 7864328 | tf_op jit(solution)/shard_map/ppermute | solution.py:229
  273.9 16.4 %collective-permute-start.39 = (bf16[2,160,4096]{2,1,0:T(8,128)(2,1)}, bf16[2,160,4096]{2,1,0:T(8,128)(2,1)}, u32[]{:S(2)}, u32[]{:S(2)}) collective-permute-start(bf16[2,160,4096]{2,1,0:T(8,128)(2,1)} %collective-permute-done.37.far_ref), channel_id=1, source_target_pairs={{0,8},{8,0},{16,24},{24,16},{1,9},{9,1},{17,25},{25,17},{2,10},{10... | collective-permute-start | bytes 7864328 | tf_op jit(solution)/shard_map/ppermute | solution.py:229
  280.6 53.1 %collective-permute-start.33 = (bf16[2,160,1024]{2,1,0:T(8,128)(2,1)}, bf16[2,160,1024]{2,1,0:T(8,128)(2,1)}, u32[]{:S(2)}, u32[]{:S(2)}) collective-permute-start(bf16[2,160,1024]{2,1,0:T(8,128)(2,1)} %collective-permute-done.31.far_ref), channel_id=1, source_target_pairs={{0,8},{8,0},{16,24},{24,16},{1,9},{9,1},{17,25},{25,17},{2,10},{10... | collective-permute-start | bytes 1966088 | tf_op jit(solution)/shard_map/ppermute | solution.py:229
  281.0 57.0 %collective-permute-start.29 = (bf16[2,160,512]{2,1,0:T(8,128)(2,1)}, bf16[2,160,512]{2,1,0:T(8,128)(2,1)}, u32[]{:S(2)}, u32[]{:S(2)}) collective-permute-start(bf16[2,160,512]{2,1,0:T(8,128)(2,1)} %send_part.19.sent_ref), channel_id=1, source_target_pairs={{0,8},{8,0},{16,24},{24,16},{1,9},{9,1},{17,25},{25,17},{2,10},{10... | collective-permute-start | bytes 983048 | tf_op jit(solution)/shard_map/ppermute | solution.py:229
  289.8 48.1 %collective-permute-start.30 = (bf16[2,160,512]{2,1,0:T(8,128)(2,1)}, bf16[2,160,512]{2,1,0:T(8,128)(2,1)}, u32[]{:S(2)}, u32[]{:S(2)}) collective-permute-start(bf16[2,160,512]{2,1,0:T(8,128)(2,1)} %collective-permute-done.28.far_ref), channel_id=1, source_target_pairs={{0,8},{8,0},{16,24},{24,16},{1,9},{9,1},{17,25},{25,17},{2,10},{10... | collective-permute-start | bytes 983048 | tf_op jit(solution)/shard_map/ppermute | solution.py:229
  289.9 50.9 %collective-permute-start.24 = (bf16[2,160,512]{2,1,0:T(8,128)(2,1)}, bf16[2,160,512]{2,1,0:T(8,128)(2,1)}, u32[]{:S(2)}, u32[]{:S(2)}) collective-permute-start(bf16[2,160,512]{2,1,0:T(8,128)(2,1)} %send_part.17.refs_0_.sent_ref), channel_id=1, source_target_pairs={{0,8},{8,0},{16,24},{24,16},{1,9},{9,1},{17,25},{25,17},{2,10},{10... | collective-permute-start | bytes 983048 | tf_op jit(solution)/shard_map/ppermute | solution.py:229
  290.3 50.5 %collective-permute-start.25 = (bf16[2,160,512]{2,1,0:T(8,128)(2,1)}, bf16[2,160,512]{2,1,0:T(8,128)(2,1)}, u32[]{:S(2)}, u32[]{:S(2)}) collective-permute-start(bf16[2,160,512]{2,1,0:T(8,128)(2,1)} %collective-permute-done.23.far_ref), channel_id=1, source_target_pairs={{0,8},{8,0},{16,24},{24,16},{1,9},{9,1},{17,25},{25,17},{2,10},{10... | collective-permute-start | bytes 983048 | tf_op jit(solution)/shard_map/ppermute | solution.py:229
  (16 other events, 113.0 us)

commit v2 on v1

v2 whole, which is shorter than its diff:
```python
import functools

import jax
import jax.numpy as jnp
from jax import lax
from jax.experimental import pallas as pl
from jax.experimental.pallas import tpu as pltpu
from jax.sharding import PartitionSpec as P


outer_rate = 0.7
nesterov_keep = 0.9
lane = 128
widest = 8
vmem_bytes = 67_043_328

first_shares = (4, 2, 2, 8, 16, 32)
raw_share = 1
last_shares = (32, 16, 8, 4, 4)

f32 = jnp.float32
bf16 = jnp.bfloat16


def chunks_of(columns, shares):
    units = columns // lane
    total = sum(shares)
    edges, seen = [0], 0
    for share in shares:
        seen += share
        edges.append(max(edges[-1], units * seen // total))
    return [(a, b - a) for a, b in zip(edges[:-1], edges[1:]) if b > a]


def step_of(start, width):
    for units in (widest, 4, 2, 1):
        if start % units == 0 and width % units == 0:
            return units
    return 1


def cores():
    return lax.axis_size("replica") // 2


def chip_core():
    r = lax.axis_index("replica")
    return r // cores(), lax.rem(r, cores())


def other(i):
    return 1 - i


def slab(far, near):
    chip, core = chip_core()
    return (other(chip) if far else chip), (other(core) if near else core)


def slab_spec(rows, step, start, far, near):
    return pl.BlockSpec(
        (1, 1, rows, step * lane),
        lambda i: (*slab(far, near), 0, start // step + i),
    )


def got_spec(rows, step, far):
    return pl.BlockSpec(
        (1, rows, step * lane), lambda i: (slab(far, False)[0], 0, i)
    )


def state_spec(rows, step, start):
    return pl.BlockSpec((rows, step * lane), lambda i: (0, start // step + i))


def half_spec(rows, step, half):
    return pl.BlockSpec((1, rows, step * lane), lambda i: (half, 0, i))


def any_spec():
    return pl.BlockSpec(memory_space=pl.ANY)


def estimate(bytes_moved):
    return pl.CostEstimate(
        flops=bytes_moved, bytes_accessed=bytes_moved, transcendentals=0
    )


def compiler_params(limit=vmem_bytes):
    return pltpu.CompilerParams(vmem_limit_bytes=limit)


def share(replicas):
    return outer_rate * (1 + nesterov_keep) / replicas


def based(replicas, params, momentum, summed):
    kept = params - (outer_rate * nesterov_keep**2) * momentum
    return (kept - share(replicas) * summed).astype(bf16)


def joined(replicas, base, summed):
    return (base.astype(f32) - share(replicas) * summed.astype(f32)).astype(bf16)


def pick_kernel(in_ref, *refs):
    refs[-1][...] = in_ref[:, 0]


def pick(delta, start, width, after):
    chips, _, rows, _ = delta.shape
    step = step_of(start, width)
    return pl.pallas_call(
        pick_kernel,
        grid=(width // step,),
        in_specs=[
            pl.BlockSpec(
                (chips, 1, rows, step * lane),
                lambda i: (0, slab(False, True)[1], 0, start // step + i),
            )
        ]
        + [any_spec()] * len(after),
        out_specs=pl.BlockSpec((chips, rows, step * lane), lambda i: (0, 0, i)),
        out_shape=pltpu.HBM((chips, rows, width * lane), bf16),
        cost_estimate=estimate(8 * rows * width * lane),
        compiler_params=compiler_params(),
        name="pick",
    )(delta, *after)


def open_kernel(near_ref, far_ref, picked_ref, raw_ref):
    picked_ref[...] = near_ref[:, 0]
    raw_ref[...] = far_ref[0]


def open_part(delta, start, width, raw_start, raw_width):
    chips, cores_, rows, _ = delta.shape
    return pl.pallas_call(
        open_kernel,
        grid=(1,),
        in_specs=[
            pl.BlockSpec(
                (chips, 1, rows, width * lane),
                lambda i: (0, slab(False, True)[1], 0, start // width),
            ),
            pl.BlockSpec(
                (1, cores_, rows, raw_width * lane),
                lambda i: (slab(True, False)[0], 0, 0, raw_start // raw_width),
            ),
        ],
        out_specs=(
            pl.BlockSpec((chips, rows, width * lane), lambda i: (0, 0, 0)),
            pl.BlockSpec((cores_, rows, raw_width * lane), lambda i: (0, 0, 0)),
        ),
        out_shape=(
            pltpu.HBM((chips, rows, width * lane), bf16),
            pltpu.HBM((cores_, rows, raw_width * lane), bf16),
        ),
        cost_estimate=estimate(8 * rows * (width + raw_width) * lane),
        compiler_params=compiler_params(),
        name="open_part",
    )(delta, delta)


def merge_kernel(raw_ref, near_raw_ref, base_ref, near_base_ref, far_ref, near_ref):
    core = slab(False, False)[1]
    for out_ref, which, base in (
        (far_ref, core, base_ref),
        (near_ref, other(core), near_base_ref),
    ):
        out_ref[0] = (
            raw_ref[which].astype(f32) + near_raw_ref[which].astype(f32)
        ).astype(bf16)
        out_ref[1] = base[0]


def merge(raw, near_raw, base, near_base):
    shape = pltpu.HBM(raw.shape, bf16)
    return pl.pallas_call(
        merge_kernel,
        out_shape=(shape, shape),
        cost_estimate=estimate(10 * base.size),
        compiler_params=compiler_params(),
        name="merge",
    )(raw, near_raw, base, near_base)


def send_kernel(
    replicas, own_ref, away_ref, got_ref, got_away_ref, params_ref, momentum_ref, out_ref
):
    out_ref[0] = (away_ref[0, 0].astype(f32) + got_away_ref[0].astype(f32)).astype(bf16)
    summed = own_ref[0, 0].astype(f32) + got_ref[0].astype(f32)
    out_ref[1] = based(replicas, params_ref[...], momentum_ref[...], summed)


def send_part(replicas, delta, got, params, momentum, start, width, limit):
    _, _, rows, _ = delta.shape
    step = step_of(start, width)
    return pl.pallas_call(
        functools.partial(send_kernel, replicas),
        grid=(width // step,),
        in_specs=[
            slab_spec(rows, step, start, False, False),
            slab_spec(rows, step, start, True, False),
            got_spec(rows, step, False),
            got_spec(rows, step, True),
            state_spec(rows, step, start),
            state_spec(rows, step, start),
        ],
        out_specs=pl.BlockSpec((2, rows, step * lane), lambda i: (0, 0, i)),
        out_shape=pltpu.HBM((2, rows, width * lane), bf16),
        cost_estimate=estimate(20 * rows * width * lane),
        compiler_params=compiler_params(limit),
        name="send_part",
    )(delta, delta, got, got, params, momentum)


def finish_kernel(replicas, own, near, *refs):
    outs = refs[-(2 * own + 1) :]
    working_ref = outs[-1]
    if own:
        (
            own_ref, got_ref, params_ref, momentum_ref,
            sent_sum, sent_base, far_sum, far_base,
        ) = refs[:8]
        refs = refs[8:]
        summed = own_ref[0, 0].astype(f32) + got_ref[0].astype(f32)
        average = (summed + far_sum[0].astype(f32)) * (1 / replicas)
        momentum_new = nesterov_keep * momentum_ref[...] + average
        outs[1][...] = momentum_new
        outs[0][...] = params_ref[...] - outer_rate * (
            average + nesterov_keep * momentum_new
        )
        working_ref[slab(False, False)] = joined(replicas, sent_base[0], far_sum[0])
        working_ref[slab(True, False)] = joined(replicas, far_base[0], sent_sum[0])
    if near:
        sent_sum, sent_base, far_sum, far_base = refs[:4]
        chip, core = slab(False, True) if own else (slab(False, False)[0], 0)
        working_ref[chip, core] = joined(replicas, sent_base[0], far_sum[0])
        working_ref[other(chip), core] = joined(replicas, far_base[0], sent_sum[0])


def finish(replicas, part, got, sent, far, near_sent, near_far, results, after, own, near):
    delta, params, momentum, start, width = part
    chips, cores_, rows, columns = delta.shape
    step = step_of(start, width)
    state = state_spec(rows, step, start)
    state_shape = jax.ShapeDtypeStruct((rows, columns), f32)
    operands, in_specs = [], []
    if own:
        operands += [delta, got, params, momentum]
        in_specs += [
            slab_spec(rows, step, start, False, False),
            got_spec(rows, step, False),
            state,
            state,
        ]
    for wanted, pair in ((own, sent), (own, far), (near, near_sent), (near, near_far)):
        if wanted:
            operands += [pair, pair]
            in_specs += [half_spec(rows, step, 0), half_spec(rows, step, 1)]
    for array in after:
        operands.append(array)
        in_specs.append(any_spec())
    aliases = {}
    if results is not None:
        for i, array in enumerate(results if own else results[-1:]):
            aliases[len(operands)] = i
            operands.append(array)
            in_specs.append(any_spec())
    count = cores_ if own else 1
    working_spec = pl.BlockSpec(
        (chips, count, rows, step * lane),
        lambda i: (0, 0 if own else slab(False, True)[1], 0, start // step + i),
    )
    working_shape = jax.ShapeDtypeStruct(delta.shape, bf16)
    outs = pl.pallas_call(
        functools.partial(finish_kernel, replicas, own, near),
        grid=(width // step,),
        in_specs=in_specs,
        out_specs=(state, state, working_spec) if own else (working_spec,),
        out_shape=(state_shape, state_shape, working_shape) if own else (working_shape,),
        input_output_aliases=aliases,
        cost_estimate=estimate((32 * own + 12 * near) * rows * width * lane),
        compiler_params=compiler_params(),
        name="finish",
    )(*operands)
    return tuple(outs) if own else (*results[:-1], outs[0])


def local(enc_delta, enc_params, enc_momentum, dec_delta, dec_params, dec_momentum):
    replicas = lax.axis_size("replica")
    near = [(r, r + 1 - 2 * (r % 2)) for r in range(replicas)]
    far = [(r, (r + replicas // 2) % replicas) for r in range(replicas)]

    def swap(x, pairs):
        return lax.ppermute(x, "replica", pairs)

    parts = []
    for block, (deltas, params, momentum, shares) in enumerate((
        (enc_delta, enc_params, enc_momentum, first_shares),
        (dec_delta, dec_params, dec_momentum, last_shares),
    )):
        _, _, rows, columns = params.shape
        delta = deltas.reshape(2, replicas // 2, rows, columns)
        params = params.reshape(rows, columns)
        momentum = momentum.reshape(rows, columns)
        chunks = chunks_of(columns, shares)
        if block == 0:
            chunks.append(chunks.pop(raw_share))
        for start, width in chunks:
            parts.append((block, (delta, params, momentum, start, width)))

    raw_at = len(first_shares) - 1
    raw_part = parts[raw_at][1]
    gots, sents, fars, near_sents = [], [], [], []
    for i, (_, part) in enumerate(parts):
        delta, params, momentum, start, width = part
        if i == 0:
            picked, raw = open_part(delta, start, width, *raw_part[3:])
        else:
            behind = [picked] if i == 2 else [sents[i - 1]]
            picked = pick(delta, start, width, behind)
        got = swap(picked, near)
        if i == 0:
            far_raw = swap(raw, far)
        sent = send_part(replicas, delta, got, params, momentum, start, width, vmem_bytes)
        out = sent
        if i == raw_at:
            out = sent[1:]
        came = swap(out, far)
        near_sent = swap(sent, near)
        gots.append(got)
        sents.append(sent)
        fars.append(came)
        near_sents.append(near_sent)

    arrays = [None, None]
    after = [sents[-1]]
    for i, (block, part) in enumerate(parts):
        came = fars[i]
        near_came = swap(came, near)
        if i == raw_at:
            near_raw = swap(far_raw, near)
            came, near_came = merge(far_raw, near_raw, came, near_came)
        last = i == len(parts) - 1
        inputs = (gots[i], sents[i], came, near_sents[i], near_came)
        arrays[block] = finish(
            replicas, part, *inputs, arrays[block], after, True, not last
        )
        if last:
            arrays[block] = finish(
                replicas, part, *inputs, arrays[block], [], False, True
            )
        after = []

    results = []
    for params_new, momentum_new, working in arrays:
        rows, columns = params_new.shape
        results.append(
            (
                params_new.reshape(1, 1, rows, columns),
                momentum_new.reshape(1, 1, rows, columns),
                working.reshape(replicas * rows, columns),
            )
        )
    return (*results[0], *results[1])


def solution(mesh):
    delta_spec = P("replica", "shard", None)
    state = P("replica", "shard", None, None)
    return jax.shard_map(
        local,
        mesh=mesh,
        in_specs=(delta_spec, state, state, delta_spec, state, state),
        out_specs=(state, state, P("shard", None), state, state, P("shard", None)),
        check_vma=False,
    )
```

time: 344 us -> 364 us (1.058)
  Pallas kernels: 110 us -> 117 us
  local copies, waits for them, and re-layouts: 0 us -> 4.01 us
  waiting for transfers between devices: 213 us -> 217 us
  starting transfers between devices: 20.4 us -> 24.1 us
    pallas_call x20 -> x24, Pallas kernels: 76.3 us -> 81.5 us  [the longest x12 54.9 us: finish(): pl.pallas_call(functools.partial(finish_kernel, replicas, own, near), gri...]
    ppermute x40 -> x46, waiting for transfers between devices: 213 us -> 217 us  [swap(): return lax.ppermute(x, 'replica', pairs)]
    ppermute x40 -> x46, starting transfers between devices: 20.4 us -> 24.1 us  [swap(): return lax.ppermute(x, 'replica', pairs)]
    pallas_call x10 -> x11, Pallas kernels: 33.5 us -> 35.3 us  [send_part(): pl.pallas_call(functools.partial(send_kernel, replicas), grid=(width // s...]
  transfers between devices with their start and end apart: 40 -> 46, of which waited for: 11 -> 18; matrix products, arithmetic and copies ran while one was open for 0% -> 0% of each run, Pallas kernels for 29% -> 22%
where the time goes in v2:
time: 364 us; the launch traced here: 362 us
  waiting for transfers between devices  217 us (60%)
  Pallas kernels  117 us (32%)
  starting transfers between devices  24.1 us (7%)
  local copies, waits for them, and re-layouts  4.01 us (1%)
    ppermute x46, waiting for transfers between devices, swap(): return lax.ppermute(x, 'replica', pairs)  217 us
    pallas_call x12, Pallas kernels, finish(): pl.pallas_call(functools.partial(finish_kernel, replicas, own, near), gri...  54.9 us
    pallas_call x11, Pallas kernels, send_part(): pl.pallas_call(functools.partial(send_kernel, replicas), grid=(width // s...  35.3 us
    ppermute x46, starting transfers between devices, swap(): return lax.ppermute(x, 'replica', pairs)  24.1 us
    pallas_call x10, Pallas kernels, pick(): pl.pallas_call(pick_kernel, grid=(width // step,), in_specs=[pl.BlockSpec...  22.9 us
  transfers between devices with their start and end apart: 46, of which 18 were waited for; matrix products, arithmetic and copies ran while one was open for 0% of the time, Pallas kernels for 22%

profile of v2, /device:TPU:0, one launch (start us, length us, event | category | flops | bytes accessed | tf_op | source)
XLA Modules:
  0.0 362.4 jit_solution(17803307598223941896)
XLA Ops:
  18.1 3.0 collective-permute-done.2.got_ref.got_away_ref.refs_1_
  21.1 3.6 send_part.13.refs_0_.refs_4_.refs_5_
  24.6 4.0 %pick.13 = bf16[2,160,4096]{2,1,0:T(8,128)(2,1)} custom-call(bf16[2,2,160,8192]{3,2,1,0:T(8,128)(2,1)} %bitcast.23, bf16[2,160,2048]{2,1,0:T(8,128)(2,1)} %send_part.13.refs_0_.refs_4_.refs_5_), custom_call_target="tpu_custom_call" | custom-call | flops 5242880 | bytes 5242880 | tf_op jit(solution)/shard_map/pick/pallas_call | solution.py:115
  29.0 4.9 %collective-permute-done.3.got_ref.got_away_ref.refs_1_ = bf16[2,160,4096]{2,1,0:T(8,128)(2,1)} collective-permute-done((bf16[2,160,4096]{2,1,0:T(8,128)(2,1)}, bf16[2,160,4096]{2,1,0:T(8,128)(2,1)}, u32[]{:S(2)}, u32[]{:S(2)}) %collective-permute-start.3) | collective-permute-done | bytes 2621472 | tf_op jit(solution)/shard_map/ppermute | solution.py:299
  33.9 6.1 %send_part.14.refs_0_.refs_4_.refs_5_ = bf16[2,160,4096]{2,1,0:T(8,128)(2,1)} custom-call(bf16[2,2,160,8192]{3,2,1,0:T(8,128)(2,1)} %bitcast.24, bf16[2,2,160,8192]{3,2,1,0:T(8,128)(2,1)} %bitcast.25, bf16[2,160,4096]{2,1,0:T(8,128)(2,1)} %collective-permute-done.3.got_ref.got_away_ref.refs_1_, ...), custom_call_target="tpu_custom_call" | custom-call | flops 13107200 | bytes 13107200 | tf_op jit(solution)/shard_map/send_part/pallas_call | solution.py:201
  45.2 4.0 %pick.15 = bf16[2,160,4096]{2,1,0:T(8,128)(2,1)} custom-call(bf16[2,2,160,8192]{3,2,1,0:T(8,128)(2,1)} %bitcast.37, bf16[2,160,256]{2,1,0:T(8,128)(2,1)} %send_part.15.refs_0_.refs_4_.refs_5_), custom_call_target="tpu_custom_call" | custom-call | flops 5242880 | bytes 5242880 | tf_op jit(solution)/shard_map/pick/pallas_call | solution.py:115
  52.2 61.1 %collective-permute-done.5.raw_ref = bf16[2,160,256]{2,1,0:T(8,128)(2,1)S(1)} collective-permute-done((bf16[2,160,256]{2,1,0:T(8,128)(2,1)}, bf16[2,160,256]{2,1,0:T(8,128)(2,1)S(1)}, u32[]{:S(2)}, u32[]{:S(2)}) %collective-permute-start.5) | collective-permute-done | bytes 163872 | tf_op jit(solution)/shard_map/ppermute | solution.py:299
  119.8 5.6 %collective-permute-done.23.refs_6_.refs_7_ = bf16[2,160,512]{2,1,0:T(8,128)(2,1)} collective-permute-done((bf16[2,160,512]{2,1,0:T(8,128)(2,1)}, bf16[2,160,512]{2,1,0:T(8,128)(2,1)}, u32[]{:S(2)}, u32[]{:S(2)}) %collective-permute-start.23) | collective-permute-done | bytes 327712 | tf_op jit(solution)/shard_map/ppermute | solution.py:299
  127.1 14.7 %collective-permute-done.20.refs_6_.refs_7_ = bf16[2,160,256]{2,1,0:T(8,128)(2,1)S(1)} collective-permute-done((bf16[2,160,256]{2,1,0:T(8,128)(2,1)}, bf16[2,160,256]{2,1,0:T(8,128)(2,1)S(1)}, u32[]{:S(2)}, u32[]{:S(2)}) %collective-permute-start.20) | collective-permute-done | bytes 163872 | tf_op jit(solution)/shard_map/ppermute | solution.py:299
  146.3 6.1 %send_part.17.refs_0_.refs_4_.refs_5_ = bf16[2,160,4096]{2,1,0:T(8,128)(2,1)} custom-call(bf16[2,2,160,8192]{3,2,1,0:T(8,128)(2,1)} %bitcast.38, bf16[2,2,160,8192]{3,2,1,0:T(8,128)(2,1)} %bitcast.39, bf16[2,160,4096]{2,1,0:T(8,128)(2,1)} %collective-permute-done.26.got_ref.got_away_ref.refs_1_, ...), custom_call_target="tpu_custom_call" | custom-call | flops 13107200 | bytes 13107200 | tf_op jit(solution)/shard_map/send_part/pallas_call | solution.py:201
  155.7 18.1 %collective-permute-done.13.refs_6_.refs_7_ = bf16[2,160,2048]{2,1,0:T(8,128)(2,1)} collective-permute-done((bf16[2,160,2048]{2,1,0:T(8,128)(2,1)}, bf16[2,160,2048]{2,1,0:T(8,128)(2,1)}, u32[]{:S(2)}, u32[]{:S(2)}) %collective-permute-start.13) | collective-permute-done | bytes 1310752 | tf_op jit(solution)/shard_map/ppermute | solution.py:299
  174.4 3.7 %send_part.18.refs_0_.refs_4_.refs_5_ = bf16[2,160,2048]{2,1,0:T(8,128)(2,1)} custom-call(bf16[2,2,160,8192]{3,2,1,0:T(8,128)(2,1)} %bitcast.41, bf16[2,2,160,8192]{3,2,1,0:T(8,128)(2,1)} %bitcast.42, bf16[2,160,2048]{2,1,0:T(8,128)(2,1)} %collective-permute-done.27.got_ref.got_away_ref.refs_1_, ...), custom_call_target="tpu_custom_call" | custom-call | flops 6553600 | bytes 6553600 | tf_op jit(solution)/shard_map/send_part/pallas_call | solution.py:201
  183.2 46.6 %collective-permute-done.7.base_ref = bf16[1,160,256]{2,1,0:T(8,128)(2,1)S(1)} collective-permute-done((bf16[1,160,256]{2,1,0:T(8,128)(2,1)S(1)}, bf16[1,160,256]{2,1,0:T(8,128)(2,1)S(1)}, u32[]{:S(2)}, u32[]{:S(2)}) %collective-permute-start.7) | collective-permute-done | bytes 81952 | tf_op jit(solution)/shard_map/ppermute | solution.py:299
  241.7 28.3 %collective-permute-done.38.refs_6_.refs_7_ = bf16[2,160,2048]{2,1,0:T(8,128)(2,1)} collective-permute-done((bf16[2,160,2048]{2,1,0:T(8,128)(2,1)}, bf16[2,160,2048]{2,1,0:T(8,128)(2,1)}, u32[]{:S(2)}, u32[]{:S(2)}) %collective-permute-start.38) | collective-permute-done | bytes 1310752 | tf_op jit(solution)/shard_map/ppermute | solution.py:299
  274.4 9.0 %collective-permute-done.35.refs_6_.refs_7_ = bf16[2,160,1024]{2,1,0:T(8,128)(2,1)} collective-permute-done((bf16[2,160,1024]{2,1,0:T(8,128)(2,1)}, bf16[2,160,1024]{2,1,0:T(8,128)(2,1)}, u32[]{:S(2)}, u32[]{:S(2)}) %collective-permute-start.35) | collective-permute-done | bytes 655392 | tf_op jit(solution)/shard_map/ppermute | solution.py:299
  289.8 8.9 %collective-permute-done.32.refs_6_.refs_7_ = bf16[2,160,512]{2,1,0:T(8,128)(2,1)} collective-permute-done((bf16[2,160,512]{2,1,0:T(8,128)(2,1)}, bf16[2,160,512]{2,1,0:T(8,128)(2,1)}, u32[]{:S(2)}, u32[]{:S(2)}) %collective-permute-start.32) | collective-permute-done | bytes 327712 | tf_op jit(solution)/shard_map/ppermute | solution.py:299
  298.6 6.4 %collective-permute-done.31.refs_6_.refs_7_ = bf16[2,160,512]{2,1,0:T(8,128)(2,1)} collective-permute-done((bf16[2,160,512]{2,1,0:T(8,128)(2,1)}, bf16[2,160,512]{2,1,0:T(8,128)(2,1)}, u32[]{:S(2)}, u32[]{:S(2)}) %collective-permute-start.31) | collective-permute-done | bytes 327712 | tf_op jit(solution)/shard_map/ppermute | solution.py:299
  312.6 4.1 %finish.14 = (f32[160,8192]{1,0:T(8,128)}, f32[160,8192]{1,0:T(8,128)}, bf16[2,2,160,8192]{3,2,1,0:T(8,128)(2,1)}) custom-call(bf16[2,2,160,8192]{3,2,1,0:T(8,128)(2,1)} %bitcast.33, bf16[2,160,1024]{2,1,0:T(8,128)(2,1)} %collective-permute-done.1.got_ref.got_away_ref.refs_1_, ...), custom_call_target="tpu_custom_call", output_to_operand_aliasing={{0}: (12, {}), {1}: (13, {}), {2}: (14, {})} | custom-call | flops 7208960 | bytes 7208960 | tf_op jit(solution)/shard_map/finish/pallas_call | solution.py:279
  316.7 5.6 %finish.15 = (f32[160,8192]{1,0:T(8,128)}, f32[160,8192]{1,0:T(8,128)}, bf16[2,2,160,8192]{3,2,1,0:T(8,128)(2,1)}) custom-call(bf16[2,2,160,8192]{3,2,1,0:T(8,128)(2,1)} %bitcast.34, bf16[2,160,2048]{2,1,0:T(8,128)(2,1)} %collective-permute-done.2.got_ref.got_away_ref.refs_1_, ...), custom_call_target="tpu_custom_call", output_to_operand_aliasing={{0}: (12, {}), {1}: (13, {}), {2}: (14, {})} | custom-call | flops 14417920 | bytes 14417920 | tf_op jit(solution)/shard_map/finish/pallas_call | solution.py:279
  322.3 10.3 %finish.16 = (f32[160,8192]{1,0:T(8,128)}, f32[160,8192]{1,0:T(8,128)}, bf16[2,2,160,8192]{3,2,1,0:T(8,128)(2,1)}) custom-call(bf16[2,2,160,8192]{3,2,1,0:T(8,128)(2,1)} %bitcast.35, bf16[2,160,4096]{2,1,0:T(8,128)(2,1)} %collective-permute-done.3.got_ref.got_away_ref.refs_1_, ...), custom_call_target="tpu_custom_call", output_to_operand_aliasing={{0}: (12, {}), {1}: (13, {}), {2}: (14, {})} | custom-call | flops 28835840 | bytes 28835840 | tf_op jit(solution)/shard_map/finish/pallas_call | solution.py:279
  334.9 10.3 %finish.18 = (f32[160,8192]{1,0:T(8,128)}, f32[160,8192]{1,0:T(8,128)}, bf16[2,2,160,8192]{3,2,1,0:T(8,128)(2,1)}) custom-call(bf16[2,2,160,8192]{3,2,1,0:T(8,128)(2,1)} %bitcast.52, bf16[2,160,4096]{2,1,0:T(8,128)(2,1)} %collective-permute-done.26.got_ref.got_away_ref.refs_1_, f32[160,8192]{1,0:T(8,128)} %bitcast.86, f32[160,8192]{1,0:T(8,128)} %bitcast.96, ...), custom_call_target="tpu_custom_call" | custom-call | flops 28835840 | bytes 28835840 | tf_op jit(solution)/shard_map/finish/pallas_call | solution.py:279
  345.2 5.6 %finish.19 = (f32[160,8192]{1,0:T(8,128)}, f32[160,8192]{1,0:T(8,128)}, bf16[2,2,160,8192]{3,2,1,0:T(8,128)(2,1)}) custom-call(bf16[2,2,160,8192]{3,2,1,0:T(8,128)(2,1)} %bitcast.53, bf16[2,160,2048]{2,1,0:T(8,128)(2,1)} %collective-permute-done.27.got_ref.got_away_ref.refs_1_, ...), custom_call_target="tpu_custom_call", output_to_operand_aliasing={{0}: (12, {}), {1}: (13, {}), {2}: (14, {})} | custom-call | flops 14417920 | bytes 14417920 | tf_op jit(solution)/shard_map/finish/pallas_call | solution.py:279
  350.8 4.1 %finish.20 = (f32[160,8192]{1,0:T(8,128)}, f32[160,8192]{1,0:T(8,128)}, bf16[2,2,160,8192]{3,2,1,0:T(8,128)(2,1)}) custom-call(bf16[2,2,160,8192]{3,2,1,0:T(8,128)(2,1)} %bitcast.54, bf16[2,160,1024]{2,1,0:T(8,128)(2,1)} %collective-permute-done.28.got_ref.got_away_ref.refs_1_, ...), custom_call_target="tpu_custom_call", output_to_operand_aliasing={{0}: (12, {}), {1}: (13, {}), {2}: (14, {})} | custom-call | flops 7208960 | bytes 7208960 | tf_op jit(solution)/shard_map/finish/pallas_call | solution.py:279
  355.0 2.9 finish.21
  (118 shorter events, 84.7 us)
Async XLA Ops:
  49.2 96.7 %collective-permute-start.26 = (bf16[2,160,4096]{2,1,0:T(8,128)(2,1)}, bf16[2,160,4096]{2,1,0:T(8,128)(2,1)}, u32[]{:S(2)}, u32[]{:S(2)}) collective-permute-start(bf16[2,160,4096]{2,1,0:T(8,128)(2,1)} %pick.15), channel_id=1, source_target_pairs={{0,8},{8,0},{16,24},{24,16},{1,9},{9,1},{17,25},{25,17},{2,10},{10... | collective-permute-start | bytes 7864328 | tf_op jit(solution)/shard_map/ppermute | solution.py:299
  49.5 124.3 %collective-permute-start.10 = (bf16[2,160,4096]{2,1,0:T(8,128)(2,1)}, bf16[2,160,4096]{2,1,0:T(8,128)(2,1)}, u32[]{:S(2)}, u32[]{:S(2)}) collective-permute-start(bf16[2,160,4096]{2,1,0:T(8,128)(2,1)} %send_part.14.refs_0_.refs_4_.refs_5_), channel_id=1, source_target_pairs={{0,16},{8,24},{16,0},{24,8},{1,17},{9,25},{17,1},{25,9},{2,18},{10... | collective-permute-start | bytes 7864328 | tf_op jit(solution)/shard_map/ppermute | solution.py:299
  52.2 61.1 %collective-permute-start.5 = (bf16[2,160,256]{2,1,0:T(8,128)(2,1)}, bf16[2,160,256]{2,1,0:T(8,128)(2,1)S(1)}, u32[]{:S(2)}, u32[]{:S(2)}) collective-permute-start(bf16[2,160,256]{2,1,0:T(8,128)(2,1)} %get-tuple-element.44), channel_id=1, source_target_pairs={{0,16},{8,24},{16,0},{24,8},{1,17},{9,25},{17,1},{25,9},{2,18},{10... | collective-permute-start | bytes 491528 | tf_op jit(solution)/shard_map/ppermute | solution.py:299
  116.9 28.9 %collective-permute-start.16 = (bf16[2,160,1024]{2,1,0:T(8,128)(2,1)}, bf16[2,160,1024]{2,1,0:T(8,128)(2,1)}, u32[]{:S(2)}, u32[]{:S(2)}) collective-permute-start(bf16[2,160,1024]{2,1,0:T(8,128)(2,1)} %send_part.12.refs_0_.refs_4_.refs_5_), channel_id=1, source_target_pairs={{0,16},{8,24},{16,0},{24,8},{1,17},{9,25},{17,1},{25,9},{2,18},{10... | collective-permute-start | bytes 1966088 | tf_op jit(solution)/shard_map/ppermute | solution.py:299
  127.1 16.5 %collective-permute-start.21 = (bf16[2,160,256]{2,1,0:T(8,128)(2,1)}, bf16[2,160,256]{2,1,0:T(8,128)(2,1)S(1)}, u32[]{:S(2)}, u32[]{:S(2)}) collective-permute-start(bf16[2,160,256]{2,1,0:T(8,128)(2,1)} %send_part.16.refs_4_.refs_5_), channel_id=1, source_target_pairs={{0,8},{8,0},{16,24},{24,16},{1,9},{9,1},{17,25},{25,17},{2,10},{10... | collective-permute-start | bytes 491528 | tf_op jit(solution)/shard_map/ppermute | solution.py:299
  141.9 32.0 %collective-permute-start.13 = (bf16[2,160,2048]{2,1,0:T(8,128)(2,1)}, bf16[2,160,2048]{2,1,0:T(8,128)(2,1)}, u32[]{:S(2)}, u32[]{:S(2)}) collective-permute-start(bf16[2,160,2048]{2,1,0:T(8,128)(2,1)} %send_part.13.refs_0_.refs_4_.refs_5_), channel_id=1, source_target_pairs={{0,16},{8,24},{16,0},{24,8},{1,17},{9,25},{17,1},{25,9},{2,18},{10... | collective-permute-start | bytes 3932168 | tf_op jit(solution)/shard_map/ppermute | solution.py:299
  154.6 19.8 %collective-permute-start.27 = (bf16[2,160,2048]{2,1,0:T(8,128)(2,1)}, bf16[2,160,2048]{2,1,0:T(8,128)(2,1)}, u32[]{:S(2)}, u32[]{:S(2)}) collective-permute-start(bf16[2,160,2048]{2,1,0:T(8,128)(2,1)} %pick.16), channel_id=1, source_target_pairs={{0,8},{8,0},{16,24},{24,16},{1,9},{9,1},{17,25},{25,17},{2,10},{10... | collective-permute-start | bytes 3932168 | tf_op jit(solution)/shard_map/ppermute | solution.py:299
  154.7 83.3 %collective-permute-start.11 = (bf16[2,160,4096]{2,1,0:T(8,128)(2,1)}, bf16[2,160,4096]{2,1,0:T(8,128)(2,1)}, u32[]{:S(2)}, u32[]{:S(2)}) collective-permute-start(bf16[2,160,4096]{2,1,0:T(8,128)(2,1)} %send_part.14.refs_0_.refs_4_.refs_5_), channel_id=1, source_target_pairs={{0,8},{8,0},{16,24},{24,16},{1,9},{9,1},{17,25},{25,17},{2,10},{10... | collective-permute-start | bytes 7864328 | tf_op jit(solution)/shard_map/ppermute | solution.py:299
  155.1 84.7 %collective-permute-start.41 = (bf16[2,160,4096]{2,1,0:T(8,128)(2,1)}, bf16[2,160,4096]{2,1,0:T(8,128)(2,1)}, u32[]{:S(2)}, u32[]{:S(2)}) collective-permute-start(bf16[2,160,4096]{2,1,0:T(8,128)(2,1)} %send_part.17.refs_0_.refs_4_.refs_5_), channel_id=1, source_target_pairs={{0,16},{8,24},{16,0},{24,8},{1,17},{9,25},{17,1},{25,9},{2,18},{10... | collective-permute-start | bytes 7864328 | tf_op jit(solution)/shard_map/ppermute | solution.py:299
  174.3 65.9 %collective-permute-start.12 = (bf16[2,160,4096]{2,1,0:T(8,128)(2,1)}, bf16[2,160,4096]{2,1,0:T(8,128)(2,1)}, u32[]{:S(2)}, u32[]{:S(2)}) collective-permute-start(bf16[2,160,4096]{2,1,0:T(8,128)(2,1)} %collective-permute-done.10.refs_6_.refs_7_), channel_id=1, source_target_pairs={{0,8},{8,0},{16,24},{24,16},{1,9},{9,1},{17,25},{25,17},{2,10},{10... | collective-permute-start | bytes 7864328 | tf_op jit(solution)/shard_map/ppermute | solution.py:299
  180.0 52.5 %collective-permute-start.28 = (bf16[2,160,1024]{2,1,0:T(8,128)(2,1)}, bf16[2,160,1024]{2,1,0:T(8,128)(2,1)}, u32[]{:S(2)}, u32[]{:S(2)}) collective-permute-start(bf16[2,160,1024]{2,1,0:T(8,128)(2,1)} %pick.17), channel_id=1, source_target_pairs={{0,8},{8,0},{16,24},{24,16},{1,9},{9,1},{17,25},{25,17},{2,10},{10... | collective-permute-start | bytes 1966088 | tf_op jit(solution)/shard_map/ppermute | solution.py:299
  181.4 48.4 %collective-permute-start.7 = (bf16[1,160,256]{2,1,0:T(8,128)(2,1)S(1)}, bf16[1,160,256]{2,1,0:T(8,128)(2,1)S(1)}, u32[]{:S(2)}, u32[]{:S(2)}) collective-permute-start(bf16[1,160,256]{2,1,0:T(8,128)(2,1)S(1)} %slice.4), channel_id=1, source_target_pairs={{0,16},{8,24},{16,0},{24,8},{1,17},{9,25},{17,1},{25,9},{2,18},{10... | collective-permute-start | bytes 245768 | tf_op jit(solution)/shard_map/ppermute | solution.py:299
  232.4 55.4 %collective-permute-start.42 = (bf16[2,160,4096]{2,1,0:T(8,128)(2,1)}, bf16[2,160,4096]{2,1,0:T(8,128)(2,1)}, u32[]{:S(2)}, u32[]{:S(2)}) collective-permute-start(bf16[2,160,4096]{2,1,0:T(8,128)(2,1)} %send_part.17.refs_0_.refs_4_.refs_5_), channel_id=1, source_target_pairs={{0,8},{8,0},{16,24},{24,16},{1,9},{9,1},{17,25},{25,17},{2,10},{10... | collective-permute-start | bytes 7864328 | tf_op jit(solution)/shard_map/ppermute | solution.py:299
  238.0 32.0 %collective-permute-start.38 = (bf16[2,160,2048]{2,1,0:T(8,128)(2,1)}, bf16[2,160,2048]{2,1,0:T(8,128)(2,1)}, u32[]{:S(2)}, u32[]{:S(2)}) collective-permute-start(bf16[2,160,2048]{2,1,0:T(8,128)(2,1)} %send_part.18.refs_0_.refs_4_.refs_5_), channel_id=1, source_target_pairs={{0,16},{8,24},{16,0},{24,8},{1,17},{9,25},{17,1},{25,9},{2,18},{10... | collective-permute-start | bytes 3932168 | tf_op jit(solution)/shard_map/ppermute | solution.py:299
  239.8 65.8 %collective-permute-start.43 = (bf16[2,160,4096]{2,1,0:T(8,128)(2,1)}, bf16[2,160,4096]{2,1,0:T(8,128)(2,1)}, u32[]{:S(2)}, u32[]{:S(2)}) collective-permute-start(bf16[2,160,4096]{2,1,0:T(8,128)(2,1)} %collective-permute-done.41.refs_6_.refs_7_), channel_id=1, source_target_pairs={{0,8},{8,0},{16,24},{24,16},{1,9},{9,1},{17,25},{25,17},{2,10},{10... | collective-permute-start | bytes 7864328 | tf_op jit(solution)/shard_map/ppermute | solution.py:299
  239.8 30.1 %collective-permute-start.39 = (bf16[2,160,2048]{2,1,0:T(8,128)(2,1)}, bf16[2,160,2048]{2,1,0:T(8,128)(2,1)}, u32[]{:S(2)}, u32[]{:S(2)}) collective-permute-start(bf16[2,160,2048]{2,1,0:T(8,128)(2,1)} %send_part.18.refs_0_.refs_4_.refs_5_), channel_id=1, source_target_pairs={{0,8},{8,0},{16,24},{24,16},{1,9},{9,1},{17,25},{25,17},{2,10},{10... | collective-permute-start | bytes 3932168 | tf_op jit(solution)/shard_map/ppermute | solution.py:299
  240.3 43.1 %collective-permute-start.35 = (bf16[2,160,1024]{2,1,0:T(8,128)(2,1)}, bf16[2,160,1024]{2,1,0:T(8,128)(2,1)}, u32[]{:S(2)}, u32[]{:S(2)}) collective-permute-start(bf16[2,160,1024]{2,1,0:T(8,128)(2,1)} %send_part.19.refs_0_.refs_4_.refs_5_), channel_id=1, source_target_pairs={{0,16},{8,24},{16,0},{24,8},{1,17},{9,25},{17,1},{25,9},{2,18},{10... | collective-permute-start | bytes 1966088 | tf_op jit(solution)/shard_map/ppermute | solution.py:299
  270.0 35.1 %collective-permute-start.40 = (bf16[2,160,2048]{2,1,0:T(8,128)(2,1)}, bf16[2,160,2048]{2,1,0:T(8,128)(2,1)}, u32[]{:S(2)}, u32[]{:S(2)}) collective-permute-start(bf16[2,160,2048]{2,1,0:T(8,128)(2,1)} %collective-permute-done.38.refs_6_.refs_7_), channel_id=1, source_target_pairs={{0,8},{8,0},{16,24},{24,16},{1,9},{9,1},{17,25},{25,17},{2,10},{10... | collective-permute-start | bytes 3932168 | tf_op jit(solution)/shard_map/ppermute | solution.py:299
  270.0 19.5 %collective-permute-start.36 = (bf16[2,160,1024]{2,1,0:T(8,128)(2,1)}, bf16[2,160,1024]{2,1,0:T(8,128)(2,1)}, u32[]{:S(2)}, u32[]{:S(2)}) collective-permute-start(bf16[2,160,1024]{2,1,0:T(8,128)(2,1)} %send_part.19.refs_0_.refs_4_.refs_5_), channel_id=1, source_target_pairs={{0,8},{8,0},{16,24},{24,16},{1,9},{9,1},{17,25},{25,17},{2,10},{10... | collective-permute-start | bytes 1966088 | tf_op jit(solution)/shard_map/ppermute | solution.py:299
  285.4 65.5 %collective-permute-start.37 = (bf16[2,160,1024]{2,1,0:T(8,128)(2,1)}, bf16[2,160,1024]{2,1,0:T(8,128)(2,1)}, u32[]{:S(2)}, u32[]{:S(2)}) collective-permute-start(bf16[2,160,1024]{2,1,0:T(8,128)(2,1)} %collective-permute-done.35.refs_6_.refs_7_), channel_id=1, source_target_pairs={{0,8},{8,0},{16,24},{24,16},{1,9},{9,1},{17,25},{25,17},{2,10},{10... | collective-permute-start | bytes 1966088 | tf_op jit(solution)/shard_map/ppermute | solution.py:299
  298.6 56.4 %collective-permute-start.33 = (bf16[2,160,512]{2,1,0:T(8,128)(2,1)}, bf16[2,160,512]{2,1,0:T(8,128)(2,1)}, u32[]{:S(2)}, u32[]{:S(2)}) collective-permute-start(bf16[2,160,512]{2,1,0:T(8,128)(2,1)} %send_part.20.refs_0_.refs_4_.refs_5_), channel_id=1, source_target_pairs={{0,8},{8,0},{16,24},{24,16},{1,9},{9,1},{17,25},{25,17},{2,10},{10... | collective-permute-start | bytes 983048 | tf_op jit(solution)/shard_map/ppermute | solution.py:299
  305.0 49.9 %collective-permute-start.34 = (bf16[2,160,512]{2,1,0:T(8,128)(2,1)}, bf16[2,160,512]{2,1,0:T(8,128)(2,1)}, u32[]{:S(2)}, u32[]{:S(2)}) collective-permute-start(bf16[2,160,512]{2,1,0:T(8,128)(2,1)} %collective-permute-done.32.refs_6_.refs_7_), channel_id=1, source_target_pairs={{0,8},{8,0},{16,24},{24,16},{1,9},{9,1},{17,25},{25,17},{2,10},{10... | collective-permute-start | bytes 983048 | tf_op jit(solution)/shard_map/ppermute | solution.py:299
  305.1 55.4 %collective-permute-start.44 = (bf16[2,160,512]{2,1,0:T(8,128)(2,1)}, bf16[2,160,512]{2,1,0:T(8,128)(2,1)}, u32[]{:S(2)}, u32[]{:S(2)}) collective-permute-start(bf16[2,160,512]{2,1,0:T(8,128)(2,1)} %send_part.21.refs_12_.refs_4_.refs_5_), channel_id=1, source_target_pairs={{0,8},{8,0},{16,24},{24,16},{1,9},{9,1},{17,25},{25,17},{2,10},{10... | collective-permute-start | bytes 983048 | tf_op jit(solution)/shard_map/ppermute | solution.py:299
  305.6 54.9 %collective-permute-start.45 = (bf16[2,160,512]{2,1,0:T(8,128)(2,1)}, bf16[2,160,512]{2,1,0:T(8,128)(2,1)}, u32[]{:S(2)}, u32[]{:S(2)}) collective-permute-start(bf16[2,160,512]{2,1,0:T(8,128)(2,1)} %collective-permute-done.31.refs_6_.refs_7_), channel_id=1, source_target_pairs={{0,8},{8,0},{16,24},{24,16},{1,9},{9,1},{17,25},{25,17},{2,10},{10... | collective-permute-start | bytes 983048 | tf_op jit(solution)/shard_map/ppermute | solution.py:299
  (29 other events, 144.2 us)

commit v3 on v2

--- a/solution.py
+++ b/solution.py
@@ -88,8 +88,8 @@
     )
 
 
-def compiler_params(limit=vmem_bytes):
-    return pltpu.CompilerParams(vmem_limit_bytes=limit)
+def compiler_params():
+    return pltpu.CompilerParams(vmem_limit_bytes=vmem_bytes)
 
 
 def share(replicas):
@@ -195,7 +195,7 @@
     out_ref[1] = based(replicas, params_ref[...], momentum_ref[...], summed)
 
 
-def send_part(replicas, delta, got, params, momentum, start, width, limit):
+def send_part(replicas, delta, got, params, momentum, start, width):
     _, _, rows, _ = delta.shape
     step = step_of(start, width)
     return pl.pallas_call(
@@ -212,7 +212,7 @@
         out_specs=pl.BlockSpec((2, rows, step * lane), lambda i: (0, 0, i)),
         out_shape=pltpu.HBM((2, rows, width * lane), bf16),
         cost_estimate=estimate(20 * rows * width * lane),
-        compiler_params=compiler_params(limit),
+        compiler_params=compiler_params(),
         name="send_part",
     )(delta, delta, got, got, params, momentum)
 
@@ -233,8 +233,10 @@
         outs[0][...] = params_ref[...] - outer_rate * (
             average + nesterov_keep * momentum_new
         )
-        working_ref[slab(False, False)] = joined(replicas, sent_base[0], far_sum[0])
-        working_ref[slab(True, False)] = joined(replicas, far_base[0], sent_sum[0])
+        chip, core = slab(False, False)
+        core = core if near else 0
+        working_ref[chip, core] = joined(replicas, sent_base[0], far_sum[0])
+        working_ref[other(chip), core] = joined(replicas, far_base[0], sent_sum[0])
     if near:
         sent_sum, sent_base, far_sum, far_base = refs[:4]
         chip, core = slab(False, True) if own else (slab(False, False)[0], 0)
@@ -270,10 +272,11 @@
             aliases[len(operands)] = i
             operands.append(array)
             in_specs.append(any_spec())
-    count = cores_ if own else 1
+    both = own and near
+    count = cores_ if both else 1
     working_spec = pl.BlockSpec(
         (chips, count, rows, step * lane),
-        lambda i: (0, 0 if own else slab(False, True)[1], 0, start // step + i),
+        lambda i: (0, 0 if both else slab(False, near)[1], 0, start // step + i),
     )
     working_shape = jax.ShapeDtypeStruct(delta.shape, bf16)
     outs = pl.pallas_call(
@@ -326,7 +329,7 @@
         got = swap(picked, near)
         if i == 0:
             far_raw = swap(raw, far)
-        sent = send_part(replicas, delta, got, params, momentum, start, width, vmem_bytes)
+        sent = send_part(replicas, delta, got, params, momentum, start, width)
         out = sent
         if i == raw_at:
             out = sent[1:]

time: 364 us -> 363 us (level)
  no operation moved by 1% of the time
where the time goes in v3:
time: 363 us; the launch traced here: 362 us
  waiting for transfers between devices  217 us (60%)
  Pallas kernels  117 us (32%)
  starting transfers between devices  24.1 us (7%)
  local copies, waits for them, and re-layouts  4.01 us (1%)
    ppermute x46, waiting for transfers between devices, swap(): return lax.ppermute(x, 'replica', pairs)  217 us
    pallas_call x12, Pallas kernels, finish(): pl.pallas_call(functools.partial(finish_kernel, replicas, own, near), gri...  54.8 us
    pallas_call x11, Pallas kernels, send_part(): pl.pallas_call(functools.partial(send_kernel, replicas), grid=(width // s...  35.3 us
    ppermute x46, starting transfers between devices, swap(): return lax.ppermute(x, 'replica', pairs)  24.1 us
    pallas_call x10, Pallas kernels, pick(): pl.pallas_call(pick_kernel, grid=(width // step,), in_specs=[pl.BlockSpec...  22.9 us
  transfers between devices with their start and end apart: 46, of which 18 were waited for; matrix products, arithmetic and copies ran while one was open for 0% of the time, Pallas kernels for 22%

profile of v3, /device:TPU:0, one launch (start us, length us, event | category | flops | bytes accessed | tf_op | source)
XLA Modules:
  0.0 362.3 jit_solution(763438509548401393)
XLA Ops:
  18.1 3.0 collective-permute-done.2.got_ref.got_away_ref.refs_1_
  21.1 3.6 send_part.13.refs_0_.refs_4_.refs_5_
  24.6 4.0 %pick.13 = bf16[2,160,4096]{2,1,0:T(8,128)(2,1)} custom-call(bf16[2,2,160,8192]{3,2,1,0:T(8,128)(2,1)} %bitcast.23, bf16[2,160,2048]{2,1,0:T(8,128)(2,1)} %send_part.13.refs_0_.refs_4_.refs_5_), custom_call_target="tpu_custom_call" | custom-call | flops 5242880 | bytes 5242880 | tf_op jit(solution)/shard_map/pick/pallas_call | solution.py:115
  29.0 4.9 %collective-permute-done.3.got_ref.got_away_ref.refs_1_ = bf16[2,160,4096]{2,1,0:T(8,128)(2,1)} collective-permute-done((bf16[2,160,4096]{2,1,0:T(8,128)(2,1)}, bf16[2,160,4096]{2,1,0:T(8,128)(2,1)}, u32[]{:S(2)}, u32[]{:S(2)}) %collective-permute-start.3) | collective-permute-done | bytes 2621472 | tf_op jit(solution)/shard_map/ppermute | solution.py:302
  33.9 6.1 %send_part.14.refs_0_.refs_4_.refs_5_ = bf16[2,160,4096]{2,1,0:T(8,128)(2,1)} custom-call(bf16[2,2,160,8192]{3,2,1,0:T(8,128)(2,1)} %bitcast.24, bf16[2,2,160,8192]{3,2,1,0:T(8,128)(2,1)} %bitcast.25, bf16[2,160,4096]{2,1,0:T(8,128)(2,1)} %collective-permute-done.3.got_ref.got_away_ref.refs_1_, ...), custom_call_target="tpu_custom_call" | custom-call | flops 13107200 | bytes 13107200 | tf_op jit(solution)/shard_map/send_part/pallas_call | solution.py:201
  45.2 4.0 %pick.15 = bf16[2,160,4096]{2,1,0:T(8,128)(2,1)} custom-call(bf16[2,2,160,8192]{3,2,1,0:T(8,128)(2,1)} %bitcast.37, bf16[2,160,256]{2,1,0:T(8,128)(2,1)} %send_part.15.refs_0_.refs_4_.refs_5_), custom_call_target="tpu_custom_call" | custom-call | flops 5242880 | bytes 5242880 | tf_op jit(solution)/shard_map/pick/pallas_call | solution.py:115
  52.2 61.1 %collective-permute-done.5.raw_ref = bf16[2,160,256]{2,1,0:T(8,128)(2,1)S(1)} collective-permute-done((bf16[2,160,256]{2,1,0:T(8,128)(2,1)}, bf16[2,160,256]{2,1,0:T(8,128)(2,1)S(1)}, u32[]{:S(2)}, u32[]{:S(2)}) %collective-permute-start.5) | collective-permute-done | bytes 163872 | tf_op jit(solution)/shard_map/ppermute | solution.py:302
  119.8 5.6 %collective-permute-done.23.refs_6_.refs_7_ = bf16[2,160,512]{2,1,0:T(8,128)(2,1)} collective-permute-done((bf16[2,160,512]{2,1,0:T(8,128)(2,1)}, bf16[2,160,512]{2,1,0:T(8,128)(2,1)}, u32[]{:S(2)}, u32[]{:S(2)}) %collective-permute-start.23) | collective-permute-done | bytes 327712 | tf_op jit(solution)/shard_map/ppermute | solution.py:302
  127.1 14.7 %collective-permute-done.20.refs_6_.refs_7_ = bf16[2,160,256]{2,1,0:T(8,128)(2,1)S(1)} collective-permute-done((bf16[2,160,256]{2,1,0:T(8,128)(2,1)}, bf16[2,160,256]{2,1,0:T(8,128)(2,1)S(1)}, u32[]{:S(2)}, u32[]{:S(2)}) %collective-permute-start.20) | collective-permute-done | bytes 163872 | tf_op jit(solution)/shard_map/ppermute | solution.py:302
  146.3 6.1 %send_part.17.refs_0_.refs_4_.refs_5_ = bf16[2,160,4096]{2,1,0:T(8,128)(2,1)} custom-call(bf16[2,2,160,8192]{3,2,1,0:T(8,128)(2,1)} %bitcast.38, bf16[2,2,160,8192]{3,2,1,0:T(8,128)(2,1)} %bitcast.39, bf16[2,160,4096]{2,1,0:T(8,128)(2,1)} %collective-permute-done.26.got_ref.got_away_ref.refs_1_, ...), custom_call_target="tpu_custom_call" | custom-call | flops 13107200 | bytes 13107200 | tf_op jit(solution)/shard_map/send_part/pallas_call | solution.py:201
  155.7 18.1 %collective-permute-done.13.refs_6_.refs_7_ = bf16[2,160,2048]{2,1,0:T(8,128)(2,1)} collective-permute-done((bf16[2,160,2048]{2,1,0:T(8,128)(2,1)}, bf16[2,160,2048]{2,1,0:T(8,128)(2,1)}, u32[]{:S(2)}, u32[]{:S(2)}) %collective-permute-start.13) | collective-permute-done | bytes 1310752 | tf_op jit(solution)/shard_map/ppermute | solution.py:302
  174.4 3.7 %send_part.18.refs_0_.refs_4_.refs_5_ = bf16[2,160,2048]{2,1,0:T(8,128)(2,1)} custom-call(bf16[2,2,160,8192]{3,2,1,0:T(8,128)(2,1)} %bitcast.41, bf16[2,2,160,8192]{3,2,1,0:T(8,128)(2,1)} %bitcast.42, bf16[2,160,2048]{2,1,0:T(8,128)(2,1)} %collective-permute-done.27.got_ref.got_away_ref.refs_1_, ...), custom_call_target="tpu_custom_call" | custom-call | flops 6553600 | bytes 6553600 | tf_op jit(solution)/shard_map/send_part/pallas_call | solution.py:201
  183.2 46.6 %collective-permute-done.7.base_ref = bf16[1,160,256]{2,1,0:T(8,128)(2,1)S(1)} collective-permute-done((bf16[1,160,256]{2,1,0:T(8,128)(2,1)S(1)}, bf16[1,160,256]{2,1,0:T(8,128)(2,1)S(1)}, u32[]{:S(2)}, u32[]{:S(2)}) %collective-permute-start.7) | collective-permute-done | bytes 81952 | tf_op jit(solution)/shard_map/ppermute | solution.py:302
  241.7 28.3 %collective-permute-done.38.refs_6_.refs_7_ = bf16[2,160,2048]{2,1,0:T(8,128)(2,1)} collective-permute-done((bf16[2,160,2048]{2,1,0:T(8,128)(2,1)}, bf16[2,160,2048]{2,1,0:T(8,128)(2,1)}, u32[]{:S(2)}, u32[]{:S(2)}) %collective-permute-start.38) | collective-permute-done | bytes 1310752 | tf_op jit(solution)/shard_map/ppermute | solution.py:302
  274.4 9.0 %collective-permute-done.35.refs_6_.refs_7_ = bf16[2,160,1024]{2,1,0:T(8,128)(2,1)} collective-permute-done((bf16[2,160,1024]{2,1,0:T(8,128)(2,1)}, bf16[2,160,1024]{2,1,0:T(8,128)(2,1)}, u32[]{:S(2)}, u32[]{:S(2)}) %collective-permute-start.35) | collective-permute-done | bytes 655392 | tf_op jit(solution)/shard_map/ppermute | solution.py:302
  289.8 8.9 %collective-permute-done.32.refs_6_.refs_7_ = bf16[2,160,512]{2,1,0:T(8,128)(2,1)} collective-permute-done((bf16[2,160,512]{2,1,0:T(8,128)(2,1)}, bf16[2,160,512]{2,1,0:T(8,128)(2,1)}, u32[]{:S(2)}, u32[]{:S(2)}) %collective-permute-start.32) | collective-permute-done | bytes 327712 | tf_op jit(solution)/shard_map/ppermute | solution.py:302
  298.6 6.4 %collective-permute-done.31.refs_6_.refs_7_ = bf16[2,160,512]{2,1,0:T(8,128)(2,1)} collective-permute-done((bf16[2,160,512]{2,1,0:T(8,128)(2,1)}, bf16[2,160,512]{2,1,0:T(8,128)(2,1)}, u32[]{:S(2)}, u32[]{:S(2)}) %collective-permute-start.31) | collective-permute-done | bytes 327712 | tf_op jit(solution)/shard_map/ppermute | solution.py:302
  312.6 4.1 %finish.14 = (f32[160,8192]{1,0:T(8,128)}, f32[160,8192]{1,0:T(8,128)}, bf16[2,2,160,8192]{3,2,1,0:T(8,128)(2,1)}) custom-call(bf16[2,2,160,8192]{3,2,1,0:T(8,128)(2,1)} %bitcast.33, bf16[2,160,1024]{2,1,0:T(8,128)(2,1)} %collective-permute-done.1.got_ref.got_away_ref.refs_1_, ...), custom_call_target="tpu_custom_call", output_to_operand_aliasing={{0}: (12, {}), {1}: (13, {}), {2}: (14, {})} | custom-call | flops 7208960 | bytes 7208960 | tf_op jit(solution)/shard_map/finish/pallas_call | solution.py:282
  316.7 5.6 %finish.15 = (f32[160,8192]{1,0:T(8,128)}, f32[160,8192]{1,0:T(8,128)}, bf16[2,2,160,8192]{3,2,1,0:T(8,128)(2,1)}) custom-call(bf16[2,2,160,8192]{3,2,1,0:T(8,128)(2,1)} %bitcast.34, bf16[2,160,2048]{2,1,0:T(8,128)(2,1)} %collective-permute-done.2.got_ref.got_away_ref.refs_1_, ...), custom_call_target="tpu_custom_call", output_to_operand_aliasing={{0}: (12, {}), {1}: (13, {}), {2}: (14, {})} | custom-call | flops 14417920 | bytes 14417920 | tf_op jit(solution)/shard_map/finish/pallas_call | solution.py:282
  322.3 10.3 %finish.16 = (f32[160,8192]{1,0:T(8,128)}, f32[160,8192]{1,0:T(8,128)}, bf16[2,2,160,8192]{3,2,1,0:T(8,128)(2,1)}) custom-call(bf16[2,2,160,8192]{3,2,1,0:T(8,128)(2,1)} %bitcast.35, bf16[2,160,4096]{2,1,0:T(8,128)(2,1)} %collective-permute-done.3.got_ref.got_away_ref.refs_1_, ...), custom_call_target="tpu_custom_call", output_to_operand_aliasing={{0}: (12, {}), {1}: (13, {}), {2}: (14, {})} | custom-call | flops 28835840 | bytes 28835840 | tf_op jit(solution)/shard_map/finish/pallas_call | solution.py:282
  334.9 10.3 %finish.18 = (f32[160,8192]{1,0:T(8,128)}, f32[160,8192]{1,0:T(8,128)}, bf16[2,2,160,8192]{3,2,1,0:T(8,128)(2,1)}) custom-call(bf16[2,2,160,8192]{3,2,1,0:T(8,128)(2,1)} %bitcast.52, bf16[2,160,4096]{2,1,0:T(8,128)(2,1)} %collective-permute-done.26.got_ref.got_away_ref.refs_1_, f32[160,8192]{1,0:T(8,128)} %bitcast.86, f32[160,8192]{1,0:T(8,128)} %bitcast.96, ...), custom_call_target="tpu_custom_call" | custom-call | flops 28835840 | bytes 28835840 | tf_op jit(solution)/shard_map/finish/pallas_call | solution.py:282
  345.2 5.6 %finish.19 = (f32[160,8192]{1,0:T(8,128)}, f32[160,8192]{1,0:T(8,128)}, bf16[2,2,160,8192]{3,2,1,0:T(8,128)(2,1)}) custom-call(bf16[2,2,160,8192]{3,2,1,0:T(8,128)(2,1)} %bitcast.53, bf16[2,160,2048]{2,1,0:T(8,128)(2,1)} %collective-permute-done.27.got_ref.got_away_ref.refs_1_, ...), custom_call_target="tpu_custom_call", output_to_operand_aliasing={{0}: (12, {}), {1}: (13, {}), {2}: (14, {})} | custom-call | flops 14417920 | bytes 14417920 | tf_op jit(solution)/shard_map/finish/pallas_call | solution.py:282
  350.8 4.1 %finish.20 = (f32[160,8192]{1,0:T(8,128)}, f32[160,8192]{1,0:T(8,128)}, bf16[2,2,160,8192]{3,2,1,0:T(8,128)(2,1)}) custom-call(bf16[2,2,160,8192]{3,2,1,0:T(8,128)(2,1)} %bitcast.54, bf16[2,160,1024]{2,1,0:T(8,128)(2,1)} %collective-permute-done.28.got_ref.got_away_ref.refs_1_, ...), custom_call_target="tpu_custom_call", output_to_operand_aliasing={{0}: (12, {}), {1}: (13, {}), {2}: (14, {})} | custom-call | flops 7208960 | bytes 7208960 | tf_op jit(solution)/shard_map/finish/pallas_call | solution.py:282
  355.0 2.9 finish.21
  (118 shorter events, 84.6 us)
Async XLA Ops:
  49.2 96.7 %collective-permute-start.26 = (bf16[2,160,4096]{2,1,0:T(8,128)(2,1)}, bf16[2,160,4096]{2,1,0:T(8,128)(2,1)}, u32[]{:S(2)}, u32[]{:S(2)}) collective-permute-start(bf16[2,160,4096]{2,1,0:T(8,128)(2,1)} %pick.15), channel_id=1, source_target_pairs={{0,8},{8,0},{16,24},{24,16},{1,9},{9,1},{17,25},{25,17},{2,10},{10... | collective-permute-start | bytes 7864328 | tf_op jit(solution)/shard_map/ppermute | solution.py:302
  49.5 124.3 %collective-permute-start.10 = (bf16[2,160,4096]{2,1,0:T(8,128)(2,1)}, bf16[2,160,4096]{2,1,0:T(8,128)(2,1)}, u32[]{:S(2)}, u32[]{:S(2)}) collective-permute-start(bf16[2,160,4096]{2,1,0:T(8,128)(2,1)} %send_part.14.refs_0_.refs_4_.refs_5_), channel_id=1, source_target_pairs={{0,16},{8,24},{16,0},{24,8},{1,17},{9,25},{17,1},{25,9},{2,18},{10... | collective-permute-start | bytes 7864328 | tf_op jit(solution)/shard_map/ppermute | solution.py:302
  52.2 61.1 %collective-permute-start.5 = (bf16[2,160,256]{2,1,0:T(8,128)(2,1)}, bf16[2,160,256]{2,1,0:T(8,128)(2,1)S(1)}, u32[]{:S(2)}, u32[]{:S(2)}) collective-permute-start(bf16[2,160,256]{2,1,0:T(8,128)(2,1)} %get-tuple-element.44), channel_id=1, source_target_pairs={{0,16},{8,24},{16,0},{24,8},{1,17},{9,25},{17,1},{25,9},{2,18},{10... | collective-permute-start | bytes 491528 | tf_op jit(solution)/shard_map/ppermute | solution.py:302
  116.9 28.9 %collective-permute-start.16 = (bf16[2,160,1024]{2,1,0:T(8,128)(2,1)}, bf16[2,160,1024]{2,1,0:T(8,128)(2,1)}, u32[]{:S(2)}, u32[]{:S(2)}) collective-permute-start(bf16[2,160,1024]{2,1,0:T(8,128)(2,1)} %send_part.12.refs_0_.refs_4_.refs_5_), channel_id=1, source_target_pairs={{0,16},{8,24},{16,0},{24,8},{1,17},{9,25},{17,1},{25,9},{2,18},{10... | collective-permute-start | bytes 1966088 | tf_op jit(solution)/shard_map/ppermute | solution.py:302
  127.1 16.5 %collective-permute-start.21 = (bf16[2,160,256]{2,1,0:T(8,128)(2,1)}, bf16[2,160,256]{2,1,0:T(8,128)(2,1)S(1)}, u32[]{:S(2)}, u32[]{:S(2)}) collective-permute-start(bf16[2,160,256]{2,1,0:T(8,128)(2,1)} %send_part.16.refs_4_.refs_5_), channel_id=1, source_target_pairs={{0,8},{8,0},{16,24},{24,16},{1,9},{9,1},{17,25},{25,17},{2,10},{10... | collective-permute-start | bytes 491528 | tf_op jit(solution)/shard_map/ppermute | solution.py:302
  141.9 32.0 %collective-permute-start.13 = (bf16[2,160,2048]{2,1,0:T(8,128)(2,1)}, bf16[2,160,2048]{2,1,0:T(8,128)(2,1)}, u32[]{:S(2)}, u32[]{:S(2)}) collective-permute-start(bf16[2,160,2048]{2,1,0:T(8,128)(2,1)} %send_part.13.refs_0_.refs_4_.refs_5_), channel_id=1, source_target_pairs={{0,16},{8,24},{16,0},{24,8},{1,17},{9,25},{17,1},{25,9},{2,18},{10... | collective-permute-start | bytes 3932168 | tf_op jit(solution)/shard_map/ppermute | solution.py:302
  154.6 19.8 %collective-permute-start.27 = (bf16[2,160,2048]{2,1,0:T(8,128)(2,1)}, bf16[2,160,2048]{2,1,0:T(8,128)(2,1)}, u32[]{:S(2)}, u32[]{:S(2)}) collective-permute-start(bf16[2,160,2048]{2,1,0:T(8,128)(2,1)} %pick.16), channel_id=1, source_target_pairs={{0,8},{8,0},{16,24},{24,16},{1,9},{9,1},{17,25},{25,17},{2,10},{10... | collective-permute-start | bytes 3932168 | tf_op jit(solution)/shard_map/ppermute | solution.py:302
  154.7 83.3 %collective-permute-start.11 = (bf16[2,160,4096]{2,1,0:T(8,128)(2,1)}, bf16[2,160,4096]{2,1,0:T(8,128)(2,1)}, u32[]{:S(2)}, u32[]{:S(2)}) collective-permute-start(bf16[2,160,4096]{2,1,0:T(8,128)(2,1)} %send_part.14.refs_0_.refs_4_.refs_5_), channel_id=1, source_target_pairs={{0,8},{8,0},{16,24},{24,16},{1,9},{9,1},{17,25},{25,17},{2,10},{10... | collective-permute-start | bytes 7864328 | tf_op jit(solution)/shard_map/ppermute | solution.py:302
  155.1 84.7 %collective-permute-start.41 = (bf16[2,160,4096]{2,1,0:T(8,128)(2,1)}, bf16[2,160,4096]{2,1,0:T(8,128)(2,1)}, u32[]{:S(2)}, u32[]{:S(2)}) collective-permute-start(bf16[2,160,4096]{2,1,0:T(8,128)(2,1)} %send_part.17.refs_0_.refs_4_.refs_5_), channel_id=1, source_target_pairs={{0,16},{8,24},{16,0},{24,8},{1,17},{9,25},{17,1},{25,9},{2,18},{10... | collective-permute-start | bytes 7864328 | tf_op jit(solution)/shard_map/ppermute | solution.py:302
  174.3 65.9 %collective-permute-start.12 = (bf16[2,160,4096]{2,1,0:T(8,128)(2,1)}, bf16[2,160,4096]{2,1,0:T(8,128)(2,1)}, u32[]{:S(2)}, u32[]{:S(2)}) collective-permute-start(bf16[2,160,4096]{2,1,0:T(8,128)(2,1)} %collective-permute-done.10.refs_6_.refs_7_), channel_id=1, source_target_pairs={{0,8},{8,0},{16,24},{24,16},{1,9},{9,1},{17,25},{25,17},{2,10},{10... | collective-permute-start | bytes 7864328 | tf_op jit(solution)/shard_map/ppermute | solution.py:302
  180.0 52.5 %collective-permute-start.28 = (bf16[2,160,1024]{2,1,0:T(8,128)(2,1)}, bf16[2,160,1024]{2,1,0:T(8,128)(2,1)}, u32[]{:S(2)}, u32[]{:S(2)}) collective-permute-start(bf16[2,160,1024]{2,1,0:T(8,128)(2,1)} %pick.17), channel_id=1, source_target_pairs={{0,8},{8,0},{16,24},{24,16},{1,9},{9,1},{17,25},{25,17},{2,10},{10... | collective-permute-start | bytes 1966088 | tf_op jit(solution)/shard_map/ppermute | solution.py:302
  181.4 48.4 %collective-permute-start.7 = (bf16[1,160,256]{2,1,0:T(8,128)(2,1)S(1)}, bf16[1,160,256]{2,1,0:T(8,128)(2,1)S(1)}, u32[]{:S(2)}, u32[]{:S(2)}) collective-permute-start(bf16[1,160,256]{2,1,0:T(8,128)(2,1)S(1)} %slice.4), channel_id=1, source_target_pairs={{0,16},{8,24},{16,0},{24,8},{1,17},{9,25},{17,1},{25,9},{2,18},{10... | collective-permute-start | bytes 245768 | tf_op jit(solution)/shard_map/ppermute | solution.py:302
  232.4 55.4 %collective-permute-start.42 = (bf16[2,160,4096]{2,1,0:T(8,128)(2,1)}, bf16[2,160,4096]{2,1,0:T(8,128)(2,1)}, u32[]{:S(2)}, u32[]{:S(2)}) collective-permute-start(bf16[2,160,4096]{2,1,0:T(8,128)(2,1)} %send_part.17.refs_0_.refs_4_.refs_5_), channel_id=1, source_target_pairs={{0,8},{8,0},{16,24},{24,16},{1,9},{9,1},{17,25},{25,17},{2,10},{10... | collective-permute-start | bytes 7864328 | tf_op jit(solution)/shard_map/ppermute | solution.py:302
  238.0 32.0 %collective-permute-start.38 = (bf16[2,160,2048]{2,1,0:T(8,128)(2,1)}, bf16[2,160,2048]{2,1,0:T(8,128)(2,1)}, u32[]{:S(2)}, u32[]{:S(2)}) collective-permute-start(bf16[2,160,2048]{2,1,0:T(8,128)(2,1)} %send_part.18.refs_0_.refs_4_.refs_5_), channel_id=1, source_target_pairs={{0,16},{8,24},{16,0},{24,8},{1,17},{9,25},{17,1},{25,9},{2,18},{10... | collective-permute-start | bytes 3932168 | tf_op jit(solution)/shard_map/ppermute | solution.py:302
  239.8 65.8 %collective-permute-start.43 = (bf16[2,160,4096]{2,1,0:T(8,128)(2,1)}, bf16[2,160,4096]{2,1,0:T(8,128)(2,1)}, u32[]{:S(2)}, u32[]{:S(2)}) collective-permute-start(bf16[2,160,4096]{2,1,0:T(8,128)(2,1)} %collective-permute-done.41.refs_6_.refs_7_), channel_id=1, source_target_pairs={{0,8},{8,0},{16,24},{24,16},{1,9},{9,1},{17,25},{25,17},{2,10},{10... | collective-permute-start | bytes 7864328 | tf_op jit(solution)/shard_map/ppermute | solution.py:302
  239.8 30.1 %collective-permute-start.39 = (bf16[2,160,2048]{2,1,0:T(8,128)(2,1)}, bf16[2,160,2048]{2,1,0:T(8,128)(2,1)}, u32[]{:S(2)}, u32[]{:S(2)}) collective-permute-start(bf16[2,160,2048]{2,1,0:T(8,128)(2,1)} %send_part.18.refs_0_.refs_4_.refs_5_), channel_id=1, source_target_pairs={{0,8},{8,0},{16,24},{24,16},{1,9},{9,1},{17,25},{25,17},{2,10},{10... | collective-permute-start | bytes 3932168 | tf_op jit(solution)/shard_map/ppermute | solution.py:302
  240.3 43.1 %collective-permute-start.35 = (bf16[2,160,1024]{2,1,0:T(8,128)(2,1)}, bf16[2,160,1024]{2,1,0:T(8,128)(2,1)}, u32[]{:S(2)}, u32[]{:S(2)}) collective-permute-start(bf16[2,160,1024]{2,1,0:T(8,128)(2,1)} %send_part.19.refs_0_.refs_4_.refs_5_), channel_id=1, source_target_pairs={{0,16},{8,24},{16,0},{24,8},{1,17},{9,25},{17,1},{25,9},{2,18},{10... | collective-permute-start | bytes 1966088 | tf_op jit(solution)/shard_map/ppermute | solution.py:302
  270.0 35.1 %collective-permute-start.40 = (bf16[2,160,2048]{2,1,0:T(8,128)(2,1)}, bf16[2,160,2048]{2,1,0:T(8,128)(2,1)}, u32[]{:S(2)}, u32[]{:S(2)}) collective-permute-start(bf16[2,160,2048]{2,1,0:T(8,128)(2,1)} %collective-permute-done.38.refs_6_.refs_7_), channel_id=1, source_target_pairs={{0,8},{8,0},{16,24},{24,16},{1,9},{9,1},{17,25},{25,17},{2,10},{10... | collective-permute-start | bytes 3932168 | tf_op jit(solution)/shard_map/ppermute | solution.py:302
  270.0 19.5 %collective-permute-start.36 = (bf16[2,160,1024]{2,1,0:T(8,128)(2,1)}, bf16[2,160,1024]{2,1,0:T(8,128)(2,1)}, u32[]{:S(2)}, u32[]{:S(2)}) collective-permute-start(bf16[2,160,1024]{2,1,0:T(8,128)(2,1)} %send_part.19.refs_0_.refs_4_.refs_5_), channel_id=1, source_target_pairs={{0,8},{8,0},{16,24},{24,16},{1,9},{9,1},{17,25},{25,17},{2,10},{10... | collective-permute-start | bytes 1966088 | tf_op jit(solution)/shard_map/ppermute | solution.py:302
  285.4 65.5 %collective-permute-start.37 = (bf16[2,160,1024]{2,1,0:T(8,128)(2,1)}, bf16[2,160,1024]{2,1,0:T(8,128)(2,1)}, u32[]{:S(2)}, u32[]{:S(2)}) collective-permute-start(bf16[2,160,1024]{2,1,0:T(8,128)(2,1)} %collective-permute-done.35.refs_6_.refs_7_), channel_id=1, source_target_pairs={{0,8},{8,0},{16,24},{24,16},{1,9},{9,1},{17,25},{25,17},{2,10},{10... | collective-permute-start | bytes 1966088 | tf_op jit(solution)/shard_map/ppermute | solution.py:302
  298.6 56.4 %collective-permute-start.33 = (bf16[2,160,512]{2,1,0:T(8,128)(2,1)}, bf16[2,160,512]{2,1,0:T(8,128)(2,1)}, u32[]{:S(2)}, u32[]{:S(2)}) collective-permute-start(bf16[2,160,512]{2,1,0:T(8,128)(2,1)} %send_part.20.refs_0_.refs_4_.refs_5_), channel_id=1, source_target_pairs={{0,8},{8,0},{16,24},{24,16},{1,9},{9,1},{17,25},{25,17},{2,10},{10... | collective-permute-start | bytes 983048 | tf_op jit(solution)/shard_map/ppermute | solution.py:302
  305.0 49.9 %collective-permute-start.34 = (bf16[2,160,512]{2,1,0:T(8,128)(2,1)}, bf16[2,160,512]{2,1,0:T(8,128)(2,1)}, u32[]{:S(2)}, u32[]{:S(2)}) collective-permute-start(bf16[2,160,512]{2,1,0:T(8,128)(2,1)} %collective-permute-done.32.refs_6_.refs_7_), channel_id=1, source_target_pairs={{0,8},{8,0},{16,24},{24,16},{1,9},{9,1},{17,25},{25,17},{2,10},{10... | collective-permute-start | bytes 983048 | tf_op jit(solution)/shard_map/ppermute | solution.py:302
  305.1 55.3 %collective-permute-start.44 = (bf16[2,160,512]{2,1,0:T(8,128)(2,1)}, bf16[2,160,512]{2,1,0:T(8,128)(2,1)}, u32[]{:S(2)}, u32[]{:S(2)}) collective-permute-start(bf16[2,160,512]{2,1,0:T(8,128)(2,1)} %send_part.21.refs_12_.refs_4_.refs_5_), channel_id=1, source_target_pairs={{0,8},{8,0},{16,24},{24,16},{1,9},{9,1},{17,25},{25,17},{2,10},{10... | collective-permute-start | bytes 983048 | tf_op jit(solution)/shard_map/ppermute | solution.py:302
  305.6 54.8 %collective-permute-start.45 = (bf16[2,160,512]{2,1,0:T(8,128)(2,1)}, bf16[2,160,512]{2,1,0:T(8,128)(2,1)}, u32[]{:S(2)}, u32[]{:S(2)}) collective-permute-start(bf16[2,160,512]{2,1,0:T(8,128)(2,1)} %collective-permute-done.31.refs_6_.refs_7_), channel_id=1, source_target_pairs={{0,8},{8,0},{16,24},{24,16},{1,9},{9,1},{17,25},{25,17},{2,10},{10... | collective-permute-start | bytes 983048 | tf_op jit(solution)/shard_map/ppermute | solution.py:302
  (29 other events, 144.2 us)

commit v4 on v3

--- a/solution.py
+++ b/solution.py
@@ -16,7 +16,8 @@
 
 first_shares = (4, 2, 2, 8, 16, 32)
 raw_share = 1
-last_shares = (32, 16, 8, 4, 4)
+last_shares = (3, 1, 4, 8, 16, 32)
+last_order = (5, 1, 4, 3, 2, 0)
 
 f32 = jnp.float32
 bf16 = jnp.bfloat16
@@ -33,7 +34,7 @@
 
 
 def step_of(start, width):
-    for units in (widest, 4, 2, 1):
+    for units in (widest, 4, 3, 2, 1):
         if start % units == 0 and width % units == 0:
             return units
     return 1
@@ -313,6 +314,8 @@
         chunks = chunks_of(columns, shares)
         if block == 0:
             chunks.append(chunks.pop(raw_share))
+        else:
+            chunks = [chunks[i] for i in last_order]
         for start, width in chunks:
             parts.append((block, (delta, params, momentum, start, width)))
 

time: 363 us -> 372 us (1.025)
  Pallas kernels: 117 us -> 122 us
    ppermute x46 -> x50, waiting for transfers between devices: 217 us -> 220 us  [swap(): return lax.ppermute(x, 'replica', pairs)]
    pallas_call x12 -> x13, Pallas kernels: 54.8 us -> 56.6 us  [finish(): pl.pallas_call(functools.partial(finish_kernel, replicas, own, near), gri...]
    pallas_call x11 -> x12, Pallas kernels: 35.3 us -> 36.9 us  [send_part(): pl.pallas_call(functools.partial(send_kernel, replicas), grid=(width // s...]
    pallas_call x10 -> x11, Pallas kernels: 22.9 us -> 24.4 us  [pick(): pl.pallas_call(pick_kernel, grid=(width // step,), in_specs=[pl.BlockSpec...]
    ppermute x46 -> x50, starting transfers between devices: 24.1 us -> 25 us  [swap(): return lax.ppermute(x, 'replica', pairs)]
  transfers between devices with their start and end apart: 46 -> 50, of which waited for: 18 -> 20; matrix products, arithmetic and copies ran while one was open for 0% -> 0% of each run, Pallas kernels for 22% -> 23%
where the time goes in v4:
time: 372 us; the launch traced here: 371 us
  waiting for transfers between devices  220 us (59%)
  Pallas kernels  122 us (33%)
  starting transfers between devices  25 us (7%)
    ppermute x50, waiting for transfers between devices, swap(): return lax.ppermute(x, 'replica', pairs)  220 us
    pallas_call x13, Pallas kernels, finish(): pl.pallas_call(functools.partial(finish_kernel, replicas, own, near), gri...  56.6 us
    pallas_call x12, Pallas kernels, send_part(): pl.pallas_call(functools.partial(send_kernel, replicas), grid=(width // s...  36.9 us
    ppermute x50, starting transfers between devices, swap(): return lax.ppermute(x, 'replica', pairs)  25 us
    pallas_call x11, Pallas kernels, pick(): pl.pallas_call(pick_kernel, grid=(width // step,), in_specs=[pl.BlockSpec...  24.4 us
  transfers between devices with their start and end apart: 50, of which 20 were waited for; matrix products, arithmetic and copies ran while one was open for 0% of the time, Pallas kernels for 23%

profile of v4, /device:TPU:0, one launch (start us, length us, event | category | flops | bytes accessed | tf_op | source)
XLA Modules:
  0.0 370.7 jit_solution(4149331591218780319)
XLA Ops:
  21.1 3.6 send_part.14.refs_0_.refs_4_.refs_5_
  24.7 4.0 %pick.14 = bf16[2,160,4096]{2,1,0:T(8,128)(2,1)} custom-call(bf16[2,2,160,8192]{3,2,1,0:T(8,128)(2,1)} %bitcast.23, bf16[2,160,2048]{2,1,0:T(8,128)(2,1)} %send_part.14.refs_0_.refs_4_.refs_5_), custom_call_target="tpu_custom_call" | custom-call | flops 5242880 | bytes 5242880 | tf_op jit(solution)/shard_map/pick/pallas_call | solution.py:116
  29.0 4.9 %collective-permute-done.3.got_ref.got_away_ref.refs_1_ = bf16[2,160,4096]{2,1,0:T(8,128)(2,1)} collective-permute-done((bf16[2,160,4096]{2,1,0:T(8,128)(2,1)}, bf16[2,160,4096]{2,1,0:T(8,128)(2,1)}, u32[]{:S(2)}, u32[]{:S(2)}) %collective-permute-start.3) | collective-permute-done | bytes 2621472 | tf_op jit(solution)/shard_map/ppermute | solution.py:303
  33.9 6.1 %send_part.15.refs_0_.refs_4_.refs_5_ = bf16[2,160,4096]{2,1,0:T(8,128)(2,1)} custom-call(bf16[2,2,160,8192]{3,2,1,0:T(8,128)(2,1)} %bitcast.24, bf16[2,2,160,8192]{3,2,1,0:T(8,128)(2,1)} %bitcast.25, bf16[2,160,4096]{2,1,0:T(8,128)(2,1)} %collective-permute-done.3.got_ref.got_away_ref.refs_1_, ...), custom_call_target="tpu_custom_call" | custom-call | flops 13107200 | bytes 13107200 | tf_op jit(solution)/shard_map/send_part/pallas_call | solution.py:202
  45.2 4.0 %pick.16 = bf16[2,160,4096]{2,1,0:T(8,128)(2,1)} custom-call(bf16[2,2,160,8192]{3,2,1,0:T(8,128)(2,1)} %bitcast.37, bf16[2,160,256]{2,1,0:T(8,128)(2,1)} %send_part.16.refs_0_.refs_4_.refs_5_), custom_call_target="tpu_custom_call" | custom-call | flops 5242880 | bytes 5242880 | tf_op jit(solution)/shard_map/pick/pallas_call | solution.py:116
  52.7 4.8 %collective-permute-done.5.raw_ref = bf16[2,160,256]{2,1,0:T(8,128)(2,1)} collective-permute-done((bf16[2,160,256]{2,1,0:T(8,128)(2,1)}, bf16[2,160,256]{2,1,0:T(8,128)(2,1)}, u32[]{:S(2)}, u32[]{:S(2)}) %collective-permute-start.5) | collective-permute-done | bytes 163872 | tf_op jit(solution)/shard_map/ppermute | solution.py:303
  61.7 6.0 %collective-permute-done.20.refs_6_.refs_7_ = bf16[2,160,256]{2,1,0:T(8,128)(2,1)S(1)} collective-permute-done((bf16[2,160,256]{2,1,0:T(8,128)(2,1)}, bf16[2,160,256]{2,1,0:T(8,128)(2,1)S(1)}, u32[]{:S(2)}, u32[]{:S(2)}) %collective-permute-start.20) | collective-permute-done | bytes 163872 | tf_op jit(solution)/shard_map/ppermute | solution.py:303
  72.5 13.8 %collective-permute-done.16.refs_6_.refs_7_ = bf16[2,160,1024]{2,1,0:T(8,128)(2,1)} collective-permute-done((bf16[2,160,1024]{2,1,0:T(8,128)(2,1)}, bf16[2,160,1024]{2,1,0:T(8,128)(2,1)}, u32[]{:S(2)}, u32[]{:S(2)}) %collective-permute-start.16) | collective-permute-done | bytes 655392 | tf_op jit(solution)/shard_map/ppermute | solution.py:303
  86.9 6.2 %send_part.18.refs_0_.refs_4_.refs_5_ = bf16[2,160,4096]{2,1,0:T(8,128)(2,1)} custom-call(bf16[2,2,160,8192]{3,2,1,0:T(8,128)(2,1)} %bitcast.38, bf16[2,2,160,8192]{3,2,1,0:T(8,128)(2,1)} %bitcast.39, bf16[2,160,4096]{2,1,0:T(8,128)(2,1)} %collective-permute-done.26.got_ref.got_away_ref.refs_1_, ...), custom_call_target="tpu_custom_call" | custom-call | flops 13107200 | bytes 13107200 | tf_op jit(solution)/shard_map/send_part/pallas_call | solution.py:202
  95.0 19.4 %collective-permute-done.13.refs_6_.refs_7_ = bf16[2,160,2048]{2,1,0:T(8,128)(2,1)} collective-permute-done((bf16[2,160,2048]{2,1,0:T(8,128)(2,1)}, bf16[2,160,2048]{2,1,0:T(8,128)(2,1)}, u32[]{:S(2)}, u32[]{:S(2)}) %collective-permute-start.13) | collective-permute-done | bytes 1310752 | tf_op jit(solution)/shard_map/ppermute | solution.py:303
  121.7 48.8 %collective-permute-done.10.refs_6_.refs_7_ = bf16[2,160,4096]{2,1,0:T(8,128)(2,1)} collective-permute-done((bf16[2,160,4096]{2,1,0:T(8,128)(2,1)}, bf16[2,160,4096]{2,1,0:T(8,128)(2,1)}, u32[]{:S(2)}, u32[]{:S(2)}) %collective-permute-start.10) | collective-permute-done | bytes 2621472 | tf_op jit(solution)/shard_map/ppermute | solution.py:303
  170.6 57.4 %collective-permute-done.7.base_ref = bf16[1,160,256]{2,1,0:T(8,128)(2,1)S(1)} collective-permute-done((bf16[1,160,256]{2,1,0:T(8,128)(2,1)S(1)}, bf16[1,160,256]{2,1,0:T(8,128)(2,1)S(1)}, u32[]{:S(2)}, u32[]{:S(2)}) %collective-permute-start.7) | collective-permute-done | bytes 81952 | tf_op jit(solution)/shard_map/ppermute | solution.py:303
  231.0 3.6 send_part.20.refs_0_.refs_4_.refs_5_
  238.5 3.3 collective-permute-done.42.refs_6_.refs_7_
  252.6 21.9 %collective-permute-done.39.refs_6_.refs_7_ = bf16[2,160,2048]{2,1,0:T(8,128)(2,1)} collective-permute-done((bf16[2,160,2048]{2,1,0:T(8,128)(2,1)}, bf16[2,160,2048]{2,1,0:T(8,128)(2,1)}, u32[]{:S(2)}, u32[]{:S(2)}) %collective-permute-start.39) | collective-permute-done | bytes 1310752 | tf_op jit(solution)/shard_map/ppermute | solution.py:303
  280.8 15.2 %collective-permute-done.36.refs_6_.refs_7_ = bf16[2,160,1024]{2,1,0:T(8,128)(2,1)} collective-permute-done((bf16[2,160,1024]{2,1,0:T(8,128)(2,1)}, bf16[2,160,1024]{2,1,0:T(8,128)(2,1)}, u32[]{:S(2)}, u32[]{:S(2)}) %collective-permute-start.36) | collective-permute-done | bytes 655392 | tf_op jit(solution)/shard_map/ppermute | solution.py:303
  300.1 6.8 %collective-permute-done.33.refs_6_.refs_7_ = bf16[2,160,512]{2,1,0:T(8,128)(2,1)} collective-permute-done((bf16[2,160,512]{2,1,0:T(8,128)(2,1)}, bf16[2,160,512]{2,1,0:T(8,128)(2,1)}, u32[]{:S(2)}, u32[]{:S(2)}) %collective-permute-start.33) | collective-permute-done | bytes 327712 | tf_op jit(solution)/shard_map/ppermute | solution.py:303
  306.9 4.8 %collective-permute-done.32.refs_6_.refs_7_ = bf16[2,160,384]{2,1,0:T(8,128)(2,1)} collective-permute-done((bf16[2,160,384]{2,1,0:T(8,128)(2,1)}, bf16[2,160,384]{2,1,0:T(8,128)(2,1)}, u32[]{:S(2)}, u32[]{:S(2)}) %collective-permute-start.32) | collective-permute-done | bytes 245792 | tf_op jit(solution)/shard_map/ppermute | solution.py:303
  319.2 4.1 %finish.15 = (f32[160,8192]{1,0:T(8,128)}, f32[160,8192]{1,0:T(8,128)}, bf16[2,2,160,8192]{3,2,1,0:T(8,128)(2,1)}) custom-call(bf16[2,2,160,8192]{3,2,1,0:T(8,128)(2,1)} %bitcast.33, bf16[2,160,1024]{2,1,0:T(8,128)(2,1)} %collective-permute-done.1.got_ref.got_away_ref.refs_1_, ...), custom_call_target="tpu_custom_call", output_to_operand_aliasing={{0}: (12, {}), {1}: (13, {}), {2}: (14, {})} | custom-call | flops 7208960 | bytes 7208960 | tf_op jit(solution)/shard_map/finish/pallas_call | solution.py:283
  323.3 5.6 %finish.16 = (f32[160,8192]{1,0:T(8,128)}, f32[160,8192]{1,0:T(8,128)}, bf16[2,2,160,8192]{3,2,1,0:T(8,128)(2,1)}) custom-call(bf16[2,2,160,8192]{3,2,1,0:T(8,128)(2,1)} %bitcast.34, bf16[2,160,2048]{2,1,0:T(8,128)(2,1)} %collective-permute-done.2.got_ref.got_away_ref.refs_1_, ...), custom_call_target="tpu_custom_call", output_to_operand_aliasing={{0}: (12, {}), {1}: (13, {}), {2}: (14, {})} | custom-call | flops 14417920 | bytes 14417920 | tf_op jit(solution)/shard_map/finish/pallas_call | solution.py:283
  328.9 10.3 %finish.17 = (f32[160,8192]{1,0:T(8,128)}, f32[160,8192]{1,0:T(8,128)}, bf16[2,2,160,8192]{3,2,1,0:T(8,128)(2,1)}) custom-call(bf16[2,2,160,8192]{3,2,1,0:T(8,128)(2,1)} %bitcast.35, bf16[2,160,4096]{2,1,0:T(8,128)(2,1)} %collective-permute-done.3.got_ref.got_away_ref.refs_1_, ...), custom_call_target="tpu_custom_call", output_to_operand_aliasing={{0}: (12, {}), {1}: (13, {}), {2}: (14, {})} | custom-call | flops 28835840 | bytes 28835840 | tf_op jit(solution)/shard_map/finish/pallas_call | solution.py:283
  341.5 10.3 %finish.19 = (f32[160,8192]{1,0:T(8,128)}, f32[160,8192]{1,0:T(8,128)}, bf16[2,2,160,8192]{3,2,1,0:T(8,128)(2,1)}) custom-call(bf16[2,2,160,8192]{3,2,1,0:T(8,128)(2,1)} %bitcast.55, bf16[2,160,4096]{2,1,0:T(8,128)(2,1)} %collective-permute-done.26.got_ref.got_away_ref.refs_1_, f32[160,8192]{1,0:T(8,128)} %bitcast.91, f32[160,8192]{1,0:T(8,128)} %bitcast.103, ...), custom_call_target="tpu_custom_call" | custom-call | flops 28835840 | bytes 28835840 | tf_op jit(solution)/shard_map/finish/pallas_call | solution.py:283
  353.7 5.8 %finish.21 = (f32[160,8192]{1,0:T(8,128)}, f32[160,8192]{1,0:T(8,128)}, bf16[2,2,160,8192]{3,2,1,0:T(8,128)(2,1)}) custom-call(bf16[2,2,160,8192]{3,2,1,0:T(8,128)(2,1)} %bitcast.57, bf16[2,160,2048]{2,1,0:T(8,128)(2,1)} %collective-permute-done.28.got_ref.got_away_ref.refs_1_, ...), custom_call_target="tpu_custom_call", output_to_operand_aliasing={{0}: (12, {}), {1}: (13, {}), {2}: (14, {})} | custom-call | flops 14417920 | bytes 14417920 | tf_op jit(solution)/shard_map/finish/pallas_call | solution.py:283
  359.5 4.1 %finish.22 = (f32[160,8192]{1,0:T(8,128)}, f32[160,8192]{1,0:T(8,128)}, bf16[2,2,160,8192]{3,2,1,0:T(8,128)(2,1)}) custom-call(bf16[2,2,160,8192]{3,2,1,0:T(8,128)(2,1)} %bitcast.58, bf16[2,160,1024]{2,1,0:T(8,128)(2,1)} %collective-permute-done.29.got_ref.got_away_ref.refs_1_, ...), custom_call_target="tpu_custom_call", output_to_operand_aliasing={{0}: (12, {}), {1}: (13, {}), {2}: (14, {})} | custom-call | flops 7208960 | bytes 7208960 | tf_op jit(solution)/shard_map/finish/pallas_call | solution.py:283
  (125 shorter events, 95.2 us)
Async XLA Ops:
  49.2 37.6 %collective-permute-start.26 = (bf16[2,160,4096]{2,1,0:T(8,128)(2,1)}, bf16[2,160,4096]{2,1,0:T(8,128)(2,1)}, u32[]{:S(2)}, u32[]{:S(2)}) collective-permute-start(bf16[2,160,4096]{2,1,0:T(8,128)(2,1)} %pick.16), channel_id=1, source_target_pairs={{0,8},{8,0},{16,24},{24,16},{1,9},{9,1},{17,25},{25,17},{2,10},{10... | collective-permute-start | bytes 7864328 | tf_op jit(solution)/shard_map/ppermute | solution.py:303
  52.6 17.5 %collective-permute-start.24 = (bf16[2,160,512]{2,1,0:T(8,128)(2,1)}, bf16[2,160,512]{2,1,0:T(8,128)(2,1)}, u32[]{:S(2)}, u32[]{:S(2)}) collective-permute-start(bf16[2,160,512]{2,1,0:T(8,128)(2,1)} %send_part.12.refs_0_.refs_4_.refs_5_), channel_id=1, source_target_pairs={{0,8},{8,0},{16,24},{24,16},{1,9},{9,1},{17,25},{25,17},{2,10},{10... | collective-permute-start | bytes 983048 | tf_op jit(solution)/shard_map/ppermute | solution.py:303
  68.4 17.9 %collective-permute-start.16 = (bf16[2,160,1024]{2,1,0:T(8,128)(2,1)}, bf16[2,160,1024]{2,1,0:T(8,128)(2,1)}, u32[]{:S(2)}, u32[]{:S(2)}) collective-permute-start(bf16[2,160,1024]{2,1,0:T(8,128)(2,1)} %send_part.13.refs_0_.refs_4_.refs_5_), channel_id=1, source_target_pairs={{0,16},{8,24},{16,0},{24,8},{1,17},{9,25},{17,1},{25,9},{2,18},{10... | collective-permute-start | bytes 1966088 | tf_op jit(solution)/shard_map/ppermute | solution.py:303
  70.3 44.0 %collective-permute-start.13 = (bf16[2,160,2048]{2,1,0:T(8,128)(2,1)}, bf16[2,160,2048]{2,1,0:T(8,128)(2,1)}, u32[]{:S(2)}, u32[]{:S(2)}) collective-permute-start(bf16[2,160,2048]{2,1,0:T(8,128)(2,1)} %send_part.14.refs_0_.refs_4_.refs_5_), channel_id=1, source_target_pairs={{0,16},{8,24},{16,0},{24,8},{1,17},{9,25},{17,1},{25,9},{2,18},{10... | collective-permute-start | bytes 3932168 | tf_op jit(solution)/shard_map/ppermute | solution.py:303
  71.0 99.5 %collective-permute-start.10 = (bf16[2,160,4096]{2,1,0:T(8,128)(2,1)}, bf16[2,160,4096]{2,1,0:T(8,128)(2,1)}, u32[]{:S(2)}, u32[]{:S(2)}) collective-permute-start(bf16[2,160,4096]{2,1,0:T(8,128)(2,1)} %send_part.15.refs_0_.refs_4_.refs_5_), channel_id=1, source_target_pairs={{0,16},{8,24},{16,0},{24,8},{1,17},{9,25},{17,1},{25,9},{2,18},{10... | collective-permute-start | bytes 7864328 | tf_op jit(solution)/shard_map/ppermute | solution.py:303
  86.3 33.7 %collective-permute-start.14 = (bf16[2,160,2048]{2,1,0:T(8,128)(2,1)}, bf16[2,160,2048]{2,1,0:T(8,128)(2,1)}, u32[]{:S(2)}, u32[]{:S(2)}) collective-permute-start(bf16[2,160,2048]{2,1,0:T(8,128)(2,1)} %send_part.14.refs_0_.refs_4_.refs_5_), channel_id=1, source_target_pairs={{0,8},{8,0},{16,24},{24,16},{1,9},{9,1},{17,25},{25,17},{2,10},{10... | collective-permute-start | bytes 3932168 | tf_op jit(solution)/shard_map/ppermute | solution.py:303
  86.8 149.9 %collective-permute-start.11 = (bf16[2,160,4096]{2,1,0:T(8,128)(2,1)}, bf16[2,160,4096]{2,1,0:T(8,128)(2,1)}, u32[]{:S(2)}, u32[]{:S(2)}) collective-permute-start(bf16[2,160,4096]{2,1,0:T(8,128)(2,1)} %send_part.15.refs_0_.refs_4_.refs_5_), channel_id=1, source_target_pairs={{0,8},{8,0},{16,24},{24,16},{1,9},{9,1},{17,25},{25,17},{2,10},{10... | collective-permute-start | bytes 7864328 | tf_op jit(solution)/shard_map/ppermute | solution.py:303
  94.6 21.5 %collective-permute-start.27 = (bf16[2,160,128]{2,1,0:T(8,128)(2,1)}, bf16[2,160,128]{2,1,0:T(8,128)(2,1)}, u32[]{:S(2)}, u32[]{:S(2)}) collective-permute-start(bf16[2,160,128]{2,1,0:T(8,128)(2,1)} %pick.17), channel_id=1, source_target_pairs={{0,8},{8,0},{16,24},{24,16},{1,9},{9,1},{17,25},{25,17},{2,10},{10... | collective-permute-start | bytes 245768 | tf_op jit(solution)/shard_map/ppermute | solution.py:303
  114.4 130.7 %collective-permute-start.45 = (bf16[2,160,4096]{2,1,0:T(8,128)(2,1)}, bf16[2,160,4096]{2,1,0:T(8,128)(2,1)}, u32[]{:S(2)}, u32[]{:S(2)}) collective-permute-start(bf16[2,160,4096]{2,1,0:T(8,128)(2,1)} %send_part.18.refs_0_.refs_4_.refs_5_), channel_id=1, source_target_pairs={{0,16},{8,24},{16,0},{24,8},{1,17},{9,25},{17,1},{25,9},{2,18},{10... | collective-permute-start | bytes 7864328 | tf_op jit(solution)/shard_map/ppermute | solution.py:303
  120.0 110.6 %collective-permute-start.28 = (bf16[2,160,2048]{2,1,0:T(8,128)(2,1)}, bf16[2,160,2048]{2,1,0:T(8,128)(2,1)}, u32[]{:S(2)}, u32[]{:S(2)}) collective-permute-start(bf16[2,160,2048]{2,1,0:T(8,128)(2,1)} %pick.18), channel_id=1, source_target_pairs={{0,8},{8,0},{16,24},{24,16},{1,9},{9,1},{17,25},{25,17},{2,10},{10... | collective-permute-start | bytes 3932168 | tf_op jit(solution)/shard_map/ppermute | solution.py:303
  121.4 106.5 %collective-permute-start.7 = (bf16[1,160,256]{2,1,0:T(8,128)(2,1)S(1)}, bf16[1,160,256]{2,1,0:T(8,128)(2,1)S(1)}, u32[]{:S(2)}, u32[]{:S(2)}) collective-permute-start(bf16[1,160,256]{2,1,0:T(8,128)(2,1)S(1)} %slice.4), channel_id=1, source_target_pairs={{0,16},{8,24},{16,0},{24,8},{1,17},{9,25},{17,1},{25,9},{2,18},{10... | collective-permute-start | bytes 245768 | tf_op jit(solution)/shard_map/ppermute | solution.py:303
  170.6 107.9 %collective-permute-start.12 = (bf16[2,160,4096]{2,1,0:T(8,128)(2,1)}, bf16[2,160,4096]{2,1,0:T(8,128)(2,1)}, u32[]{:S(2)}, u32[]{:S(2)}) collective-permute-start(bf16[2,160,4096]{2,1,0:T(8,128)(2,1)} %collective-permute-done.10.refs_6_.refs_7_), channel_id=1, source_target_pairs={{0,8},{8,0},{16,24},{24,16},{1,9},{9,1},{17,25},{25,17},{2,10},{10... | collective-permute-start | bytes 7864328 | tf_op jit(solution)/shard_map/ppermute | solution.py:303
  230.5 48.5 %collective-permute-start.46 = (bf16[2,160,4096]{2,1,0:T(8,128)(2,1)}, bf16[2,160,4096]{2,1,0:T(8,128)(2,1)}, u32[]{:S(2)}, u32[]{:S(2)}) collective-permute-start(bf16[2,160,4096]{2,1,0:T(8,128)(2,1)} %send_part.18.refs_0_.refs_4_.refs_5_), channel_id=1, source_target_pairs={{0,8},{8,0},{16,24},{24,16},{1,9},{9,1},{17,25},{25,17},{2,10},{10... | collective-permute-start | bytes 7864328 | tf_op jit(solution)/shard_map/ppermute | solution.py:303
  243.4 31.2 %collective-permute-start.39 = (bf16[2,160,2048]{2,1,0:T(8,128)(2,1)}, bf16[2,160,2048]{2,1,0:T(8,128)(2,1)}, u32[]{:S(2)}, u32[]{:S(2)}) collective-permute-start(bf16[2,160,2048]{2,1,0:T(8,128)(2,1)} %send_part.20.refs_0_.refs_4_.refs_5_), channel_id=1, source_target_pairs={{0,16},{8,24},{16,0},{24,8},{1,17},{9,25},{17,1},{25,9},{2,18},{10... | collective-permute-start | bytes 3932168 | tf_op jit(solution)/shard_map/ppermute | solution.py:303
  245.1 67.1 %collective-permute-start.47 = (bf16[2,160,4096]{2,1,0:T(8,128)(2,1)}, bf16[2,160,4096]{2,1,0:T(8,128)(2,1)}, u32[]{:S(2)}, u32[]{:S(2)}) collective-permute-start(bf16[2,160,4096]{2,1,0:T(8,128)(2,1)} %collective-permute-done.45.refs_6_.refs_7_), channel_id=1, source_target_pairs={{0,8},{8,0},{16,24},{24,16},{1,9},{9,1},{17,25},{25,17},{2,10},{10... | collective-permute-start | bytes 7864328 | tf_op jit(solution)/shard_map/ppermute | solution.py:303
  252.5 43.5 %collective-permute-start.40 = (bf16[2,160,2048]{2,1,0:T(8,128)(2,1)}, bf16[2,160,2048]{2,1,0:T(8,128)(2,1)}, u32[]{:S(2)}, u32[]{:S(2)}) collective-permute-start(bf16[2,160,2048]{2,1,0:T(8,128)(2,1)} %send_part.20.refs_0_.refs_4_.refs_5_), channel_id=1, source_target_pairs={{0,8},{8,0},{16,24},{24,16},{1,9},{9,1},{17,25},{25,17},{2,10},{10... | collective-permute-start | bytes 3932168 | tf_op jit(solution)/shard_map/ppermute | solution.py:303
  274.5 37.1 %collective-permute-start.41 = (bf16[2,160,2048]{2,1,0:T(8,128)(2,1)}, bf16[2,160,2048]{2,1,0:T(8,128)(2,1)}, u32[]{:S(2)}, u32[]{:S(2)}) collective-permute-start(bf16[2,160,2048]{2,1,0:T(8,128)(2,1)} %collective-permute-done.39.refs_6_.refs_7_), channel_id=1, source_target_pairs={{0,8},{8,0},{16,24},{24,16},{1,9},{9,1},{17,25},{25,17},{2,10},{10... | collective-permute-start | bytes 3932168 | tf_op jit(solution)/shard_map/ppermute | solution.py:303
  278.9 17.0 %collective-permute-start.36 = (bf16[2,160,1024]{2,1,0:T(8,128)(2,1)}, bf16[2,160,1024]{2,1,0:T(8,128)(2,1)}, u32[]{:S(2)}, u32[]{:S(2)}) collective-permute-start(bf16[2,160,1024]{2,1,0:T(8,128)(2,1)} %send_part.21.refs_0_.refs_4_.refs_5_), channel_id=1, source_target_pairs={{0,16},{8,24},{16,0},{24,8},{1,17},{9,25},{17,1},{25,9},{2,18},{10... | collective-permute-start | bytes 1966088 | tf_op jit(solution)/shard_map/ppermute | solution.py:303
  280.7 19.1 %collective-permute-start.37 = (bf16[2,160,1024]{2,1,0:T(8,128)(2,1)}, bf16[2,160,1024]{2,1,0:T(8,128)(2,1)}, u32[]{:S(2)}, u32[]{:S(2)}) collective-permute-start(bf16[2,160,1024]{2,1,0:T(8,128)(2,1)} %send_part.21.refs_0_.refs_4_.refs_5_), channel_id=1, source_target_pairs={{0,8},{8,0},{16,24},{24,16},{1,9},{9,1},{17,25},{25,17},{2,10},{10... | collective-permute-start | bytes 1966088 | tf_op jit(solution)/shard_map/ppermute | solution.py:303
  295.9 63.5 %collective-permute-start.38 = (bf16[2,160,1024]{2,1,0:T(8,128)(2,1)}, bf16[2,160,1024]{2,1,0:T(8,128)(2,1)}, u32[]{:S(2)}, u32[]{:S(2)}) collective-permute-start(bf16[2,160,1024]{2,1,0:T(8,128)(2,1)} %collective-permute-done.36.refs_6_.refs_7_), channel_id=1, source_target_pairs={{0,8},{8,0},{16,24},{24,16},{1,9},{9,1},{17,25},{25,17},{2,10},{10... | collective-permute-start | bytes 1966088 | tf_op jit(solution)/shard_map/ppermute | solution.py:303
  306.9 56.8 %collective-permute-start.34 = (bf16[2,160,512]{2,1,0:T(8,128)(2,1)}, bf16[2,160,512]{2,1,0:T(8,128)(2,1)}, u32[]{:S(2)}, u32[]{:S(2)}) collective-permute-start(bf16[2,160,512]{2,1,0:T(8,128)(2,1)} %send_part.22.refs_0_.refs_4_.refs_5_), channel_id=1, source_target_pairs={{0,8},{8,0},{16,24},{24,16},{1,9},{9,1},{17,25},{25,17},{2,10},{10... | collective-permute-start | bytes 983048 | tf_op jit(solution)/shard_map/ppermute | solution.py:303
  311.7 52.0 %collective-permute-start.35 = (bf16[2,160,512]{2,1,0:T(8,128)(2,1)}, bf16[2,160,512]{2,1,0:T(8,128)(2,1)}, u32[]{:S(2)}, u32[]{:S(2)}) collective-permute-start(bf16[2,160,512]{2,1,0:T(8,128)(2,1)} %collective-permute-done.33.refs_6_.refs_7_), channel_id=1, source_target_pairs={{0,8},{8,0},{16,24},{24,16},{1,9},{9,1},{17,25},{25,17},{2,10},{10... | collective-permute-start | bytes 983048 | tf_op jit(solution)/shard_map/ppermute | solution.py:303
  311.7 57.1 %collective-permute-start.48 = (bf16[2,160,384]{2,1,0:T(8,128)(2,1)}, bf16[2,160,384]{2,1,0:T(8,128)(2,1)}, u32[]{:S(2)}, u32[]{:S(2)}) collective-permute-start(bf16[2,160,384]{2,1,0:T(8,128)(2,1)} %send_part.23.refs_12_.refs_4_.refs_5_), channel_id=1, source_target_pairs={{0,8},{8,0},{16,24},{24,16},{1,9},{9,1},{17,25},{25,17},{2,10},{10... | collective-permute-start | bytes 737288 | tf_op jit(solution)/shard_map/ppermute | solution.py:303
  312.2 56.6 %collective-permute-start.49 = (bf16[2,160,384]{2,1,0:T(8,128)(2,1)}, bf16[2,160,384]{2,1,0:T(8,128)(2,1)}, u32[]{:S(2)}, u32[]{:S(2)}) collective-permute-start(bf16[2,160,384]{2,1,0:T(8,128)(2,1)} %collective-permute-done.32.refs_6_.refs_7_), channel_id=1, source_target_pairs={{0,8},{8,0},{16,24},{24,16},{1,9},{9,1},{17,25},{25,17},{2,10},{10... | collective-permute-start | bytes 737288 | tf_op jit(solution)/shard_map/ppermute | solution.py:303
  (31 other events, 156.2 us)
